TPU v7x, 32 devices: a whole 2x2x4 slice. The times are simulated.
32 devices in a mesh: dp: 8 (over z, y), seq: 4 (over x, core).
Axes of the slice: x: 2, y: 2, z: 4, core: 2. Of those that a mesh axis runs over, the one named last changes fastest.
Arguments:
- hidden_in: bfloat16 [16, 2048, 768], P('dp', 'seq'), may hold values from -6 to 6
- seg_lengths: int32 [16, 16], P('dp'), may hold values from 1 to 1024, 2048 in all within a row
- query_weight: bfloat16 [768, 768], replicated, may hold values from -0.3125 to 0.3125
- query_bias: float32 [768], replicated, may hold values from -3 to 3
- key_weight: bfloat16 [768, 768], replicated, may hold values from -0.21875 to 0.21875
- value_weight: bfloat16 [768, 768], replicated, may hold values from -0.21875 to 0.21875
- value_bias: float32 [768], replicated, may hold values from -3 to 3
- out_weight: bfloat16 [768, 768], replicated, may hold values from -0.875 to 0.875
- out_bias: float32 [768], replicated, may hold values from -3 to 3
- first_gain: float32 [768], replicated, may hold values from 0.5 to 1.5
- first_shift: float32 [768], replicated, may hold values from -2 to 2
- up_weight: bfloat16 [768, 3072], replicated, may hold values from -0.21875 to 0.21875
- up_bias: float32 [3072], replicated, may hold values from -3 to 3
- down_weight: bfloat16 [3072, 768], replicated, may hold values from -0.15625 to 0.15625
- down_bias: float32 [768], replicated, may hold values from -3 to 3
- second_gain: float32 [768], replicated, may hold values from 0.5 to 1.5
- second_shift: float32 [768], replicated, may hold values from -2 to 2
- cot_out: bfloat16 [16, 2048, 768], P('dp', 'seq'), may hold values from -6 to 6
- cot_pool: float32 [16, 15, 768], P('dp'), may hold values from -15 to 15
Outputs:
- layer_out: bfloat16 [16, 2048, 768], P('dp', 'seq')
- pooled: float32 [16, 15, 768], P('dp')
- grad_hidden: float32 [16, 2048, 768], P('dp', 'seq')
- grad_query_weight: float32 [768, 768], replicated
- grad_query_bias: float32 [768], replicated
- grad_key_weight: float32 [768, 768], replicated
- grad_value_weight: float32 [768, 768], replicated
- grad_value_bias: float32 [768], replicated
- grad_out_weight: float32 [768, 768], replicated
- grad_out_bias: float32 [768], replicated
- grad_first_gain: float32 [768], replicated
- grad_first_shift: float32 [768], replicated
- grad_up_weight: float32 [768, 3072], replicated
- grad_up_bias: float32 [3072], replicated
- grad_down_weight: float32 [3072, 768], replicated
- grad_down_bias: float32 [768], replicated
- grad_second_gain: float32 [768], replicated
- grad_second_shift: float32 [768], replicated
Inputs may be any that keep to these rules, and one draw needn't show every extreme that they name: `seg_lengths`: a row's 16 entries add up to 2048; the last one is the row's padding; in every row some entry equals 1024.
All inputs are finite; a program needn't handle non-finite values.
Results may differ from a plain program's by a relative error of at most 0.015.
Values may be sent and summed in bfloat16 or wider, within the bound.
No kernel may reach another device: no remote copies, remote signals or barrier semaphores. Data moves between devices by JAX's collectives and lax.ppermute only.
A program may use at most 448 MiB of HBM per device.

v0:
```python
import jax
import jax.numpy as jnp
from jax import lax
from jax.sharding import PartitionSpec as P

H = 12
HD = 64
MICRO = 2
NSENT = 15


EPS = 1e-06
HIGH = lax.Precision.HIGHEST


def layer_norm(hidden, norm_gain, norm_shift):
    centred = hidden - jnp.mean(hidden, axis=-1, keepdims=True)
    spread = jnp.mean(centred * centred, axis=-1, keepdims=True)
    return centred * lax.rsqrt(spread + EPS) * norm_gain + norm_shift


def gelu_exact(values):
    return jax.nn.gelu(values, approximate=False)


def project(activations, weight):
    return jnp.einsum("rtd,de->rte", activations, weight, preferred_element_type=jnp.float32)


def project_back(gradients, weight):
    return jnp.einsum("rte,de->rtd", gradients, weight, preferred_element_type=jnp.float32)


def weight_grad(activations, gradients):
    return jnp.einsum("rtd,rte->de", activations, gradients, preferred_element_type=jnp.float32)


def column_sum(gradients):
    return jnp.sum(gradients.astype(jnp.float32), axis=(0, 1))


def segment_of(places, segment_ends):
    return jnp.sum((places[None, :, None] >= segment_ends[:, None, :]).astype(jnp.int32), axis=2)


def masked_scores(query_heads, key_heads, same_segment):
    scores = (
        jnp.einsum("rqhd,rkhd->rhqk", query_heads, key_heads, preferred_element_type=jnp.float32)
        * 0.125
    )
    return jnp.where(same_segment, scores, -1e30)


def local(
    hidden_in,
    seg_lengths,
    query_weight,
    query_bias,
    key_weight,
    value_weight,
    value_bias,
    out_weight,
    out_bias,
    first_gain,
    first_shift,
    up_weight,
    up_bias,
    down_weight,
    down_bias,
    second_gain,
    second_shift,
    cot_out,
    cot_pool,
):
    rows_dev, local_len, model_width = hidden_in.shape
    row_length = local_len * lax.axis_size("seq")
    block_rows = rows_dev // MICRO
    segment_ends = jnp.cumsum(seg_lengths, axis=1)
    sentence_sizes = seg_lengths[:, :NSENT].astype(jnp.float32)
    own_places = lax.axis_index("seq") * local_len + jnp.arange(local_len, dtype=jnp.int32)
    own_segment = segment_of(own_places, segment_ends)
    row_segment = segment_of(jnp.arange(row_length, dtype=jnp.int32), segment_ends)
    membership = (own_segment[:, :, None] == jnp.arange(NSENT, dtype=jnp.int32)).astype(jnp.float32)
    pool_weights = cot_pool / sentence_sizes[:, :, None]
    finals = []
    pool_parts = []
    input_grads = []
    grad_totals = None
    for micro_index in range(MICRO):
        row_span = slice(micro_index * block_rows, (micro_index + 1) * block_rows)
        inputs = hidden_in[row_span]
        same_segment = (
            own_segment[row_span][:, None, :, None] == row_segment[row_span][:, None, None, :]
        )
        queries = (project(inputs, query_weight) + query_bias).astype(jnp.bfloat16)
        keys_own = project(inputs, key_weight).astype(jnp.bfloat16)
        values_own = (project(inputs, value_weight) + value_bias).astype(jnp.bfloat16)
        keys_row, values_row = (
            lax.all_gather(keys_own, "seq", axis=1, tiled=True),
            lax.all_gather(values_own, "seq", axis=1, tiled=True),
        )
        query_heads = queries.reshape(block_rows, local_len, H, HD)
        key_heads = keys_row.reshape(block_rows, row_length, H, HD)
        value_heads = values_row.reshape(block_rows, row_length, H, HD)
        scores = masked_scores(query_heads, key_heads, same_segment)
        row_max = jnp.max(scores, axis=3, keepdims=True)
        row_total = jnp.sum(jnp.exp(scores - row_max), axis=3, keepdims=True)
        log_total = row_max + jnp.log(row_total)
        probs_low = jnp.exp(scores - log_total).astype(jnp.bfloat16)
        attended = jnp.einsum(
            "rhqk,rkhd->rqhd", probs_low, value_heads, preferred_element_type=jnp.float32
        )
        attended = attended.reshape(block_rows, local_len, model_width).astype(jnp.bfloat16)
        first_sum = inputs.astype(jnp.float32) + project(attended, out_weight) + out_bias
        normed, first_back = jax.vjp(layer_norm, first_sum, first_gain, first_shift)
        normed_low = normed.astype(jnp.bfloat16)
        pre_act = project(normed_low, up_weight) + up_bias
        activated, gelu_back = jax.vjp(gelu_exact, pre_act)
        activated_low = activated.astype(jnp.bfloat16)
        second_sum = normed + project(activated_low, down_weight) + down_bias
        final_norm, second_back = jax.vjp(layer_norm, second_sum, second_gain, second_shift)
        finals.append(final_norm.astype(jnp.bfloat16))
        pool_parts.append(
            jnp.einsum(
                "rts,rtd->rsd",
                membership[row_span],
                final_norm,
                precision=HIGH,
                preferred_element_type=jnp.float32,
            )
        )
        upstream = cot_out[row_span].astype(jnp.float32) + jnp.einsum(
            "rts,rsd->rtd",
            membership[row_span],
            pool_weights[row_span],
            precision=HIGH,
            preferred_element_type=jnp.float32,
        )
        d_second, d_gain_two, d_shift_two = second_back(upstream)
        d_branch = d_second.astype(jnp.bfloat16)
        (d_pre,) = gelu_back(project_back(d_branch, down_weight))
        d_pre_low = d_pre.astype(jnp.bfloat16)
        d_normed = d_second + project_back(d_pre_low, up_weight)
        d_first, d_gain_one, d_shift_one = first_back(d_normed)
        d_attn_out = d_first.astype(jnp.bfloat16)
        d_attended = project_back(d_attn_out, out_weight).astype(jnp.bfloat16)
        d_attended = d_attended.reshape(block_rows, local_len, H, HD)
        scores_again = masked_scores(query_heads, key_heads, same_segment)
        soft = jnp.exp(scores_again - log_total)
        soft_low = soft.astype(jnp.bfloat16)
        d_soft = jnp.einsum(
            "rqhd,rkhd->rhqk", d_attended, value_heads, preferred_element_type=jnp.float32
        )
        d_scores = (soft * (d_soft - jnp.sum(soft * d_soft, axis=3, keepdims=True))).astype(
            jnp.bfloat16
        )
        d_query = (
            jnp.einsum("rhqk,rkhd->rqhd", d_scores, key_heads, preferred_element_type=jnp.float32)
            * 0.125
        )
        d_query = d_query.reshape(block_rows, local_len, model_width).astype(jnp.bfloat16)
        d_key_row = (
            jnp.einsum("rhqk,rqhd->rkhd", d_scores, query_heads, preferred_element_type=jnp.float32)
            * 0.125
        )
        d_key_row = d_key_row.reshape(block_rows, row_length, model_width)
        d_value_row = jnp.einsum(
            "rhqk,rqhd->rkhd", soft_low, d_attended, preferred_element_type=jnp.float32
        )
        d_value_row = d_value_row.reshape(block_rows, row_length, model_width)
        d_key_sum, d_value_sum = (
            lax.psum_scatter(d_key_row, "seq", scatter_dimension=1, tiled=True),
            lax.psum_scatter(d_value_row, "seq", scatter_dimension=1, tiled=True),
        )
        d_keys = d_key_sum.astype(jnp.bfloat16)
        d_values = d_value_sum.astype(jnp.bfloat16)
        input_grads.append(
            d_first
            + project_back(d_query, query_weight)
            + project_back(d_keys, key_weight)
            + project_back(d_values, value_weight)
        )
        grad_terms = (
            weight_grad(inputs, d_query),
            column_sum(d_query),
            weight_grad(inputs, d_keys),
            weight_grad(inputs, d_values),
            column_sum(d_values),
            weight_grad(attended, d_attn_out),
            column_sum(d_attn_out),
            d_gain_one,
            d_shift_one,
            weight_grad(normed_low, d_pre_low),
            column_sum(d_pre_low),
            weight_grad(activated_low, d_branch),
            column_sum(d_branch),
            d_gain_two,
            d_shift_two,
        )
        grad_totals = (
            grad_terms if micro_index == 0 else jax.tree.map(jnp.add, grad_totals, grad_terms)
        )
    layer_out = jnp.concatenate(finals, axis=0)
    grad_hidden = jnp.concatenate(input_grads, axis=0)
    pooled = lax.psum(jnp.concatenate(pool_parts, axis=0).astype(jnp.bfloat16), "seq").astype(
        jnp.float32
    )
    pooled = pooled / sentence_sizes[:, :, None]
    small_order = (1, 4, 6, 7, 8, 10, 12, 13, 14)
    small_grads = jnp.concatenate([grad_totals[position] for position in small_order])
    query_flat = grad_totals[0].reshape(-1)
    key_flat = grad_totals[2].reshape(-1)
    value_flat = grad_totals[3].reshape(-1)
    out_flat = grad_totals[5].reshape(-1)
    up_flat = grad_totals[9].reshape(-1)
    down_flat = grad_totals[11].reshape(-1)
    query_part, key_part, value_part, out_part, up_part, down_part, small_part = (
        lax.psum_scatter(query_flat, ("dp", "seq"), scatter_dimension=0, tiled=True),
        lax.psum_scatter(key_flat, ("dp", "seq"), scatter_dimension=0, tiled=True),
        lax.psum_scatter(value_flat, ("dp", "seq"), scatter_dimension=0, tiled=True),
        lax.psum_scatter(out_flat, ("dp", "seq"), scatter_dimension=0, tiled=True),
        lax.psum_scatter(up_flat, ("dp", "seq"), scatter_dimension=0, tiled=True),
        lax.psum_scatter(down_flat, ("dp", "seq"), scatter_dimension=0, tiled=True),
        lax.psum_scatter(small_grads, ("dp", "seq"), scatter_dimension=0, tiled=True),
    )
    query_all, key_all, value_all, out_all, up_all, down_all, small_all = (
        lax.all_gather(query_part.astype(jnp.bfloat16), ("dp", "seq"), axis=0, tiled=True).astype(
            query_part.dtype
        ),
        lax.all_gather(key_part.astype(jnp.bfloat16), ("dp", "seq"), axis=0, tiled=True).astype(
            key_part.dtype
        ),
        lax.all_gather(value_part.astype(jnp.bfloat16), ("dp", "seq"), axis=0, tiled=True).astype(
            value_part.dtype
        ),
        lax.all_gather(out_part.astype(jnp.bfloat16), ("dp", "seq"), axis=0, tiled=True).astype(
            out_part.dtype
        ),
        lax.all_gather(up_part.astype(jnp.bfloat16), ("dp", "seq"), axis=0, tiled=True).astype(
            up_part.dtype
        ),
        lax.all_gather(down_part.astype(jnp.bfloat16), ("dp", "seq"), axis=0, tiled=True).astype(
            down_part.dtype
        ),
        lax.all_gather(small_part.astype(jnp.bfloat16), ("dp", "seq"), axis=0, tiled=True).astype(
            small_part.dtype
        ),
    )
    hidden_units = up_weight.shape[1]
    small_sizes = (
        model_width,
        model_width,
        model_width,
        model_width,
        model_width,
        hidden_units,
        model_width,
        model_width,
        model_width,
    )
    small_pieces = []
    offset = 0
    for piece_size in small_sizes:
        small_pieces.append(small_all[offset : offset + piece_size])
        offset = offset + piece_size
    return (
        layer_out,
        pooled,
        grad_hidden,
        query_all.reshape(query_weight.shape),
        small_pieces[0],
        key_all.reshape(key_weight.shape),
        value_all.reshape(value_weight.shape),
        small_pieces[1],
        out_all.reshape(out_weight.shape),
        small_pieces[2],
        small_pieces[3],
        small_pieces[4],
        up_all.reshape(up_weight.shape),
        small_pieces[5],
        down_all.reshape(down_weight.shape),
        small_pieces[6],
        small_pieces[7],
        small_pieces[8],
    )


def solution(mesh):
    placed = (
        P("dp", "seq", None),
        P("dp", None),
        P(),
        P(),
        P(),
        P(),
        P(),
        P(),
        P(),
        P(),
        P(),
        P(),
        P(),
        P(),
        P(),
        P(),
        P(),
        P("dp", "seq", None),
        P("dp", None, None),
    )
    return jax.shard_map(
        local,
        mesh=mesh,
        in_specs=placed,
        out_specs=(
            P("dp", "seq", None),
            P("dp", None, None),
            P("dp", "seq", None),
            P(),
            P(),
            P(),
            P(),
            P(),
            P(),
            P(),
            P(),
            P(),
            P(),
            P(),
            P(),
            P(),
            P(),
            P(),
        ),
        check_vma=False,
    )
```

profile of v0, /device:TPU:0, one launch (start us, length us, event | category | flops | bytes accessed | tf_op | source)
XLA Modules:
  0.0 1500.0 jit_solution(17569260541239695951)
XLA Ops:
  46.9 22.1 %fusion.1 = (f32[12,512]{1,0:T(8,128)S(1)}, f32[12,512,2048]{2,1,0:T(8,128)}) fusion(pred[512,2048]{1,0:T(8,128)(4,1)S(1)} %broadcast_compare_fusion, bf16[512,12,64]{0,2,1:T(8,128)(2,1)} %bitcast.298, bf16[2048,12,64]{0,2,1:T(8,128)(2,1)} %bitcast.287), kind=kOutput, calls=%fused_computation.11 | convolution fusion | flops 1648355328 | bytes 55336960 | tf_op jit(solution)/shard_map/rqhd,rkhd->rhqk/dot_general | solution.py:48
  69.0 22.4 %exponential_reduce_fusion = f32[12,512]{1,0:T(8,128)S(1)} fusion(f32[12,512,2048]{2,1,0:T(8,128)} %get-tuple-element.163, f32[12,512]{1,0:T(8,128)S(1)} %get-tuple-element.162, pred[512,2048]{1,0:T(8,128)(4,1)S(1)} %broadcast_compare_fusion), kind=kLoop, calls=%fused_computation.5 | loop fusion | flops 50325504 | bytes 51429376 | tf_op jit(solution)/shard_map/reduce_sum | solution.py:107
  96.1 21.6 %convolution_convert_fusion = bf16[12,64,512]{2,1,0:T(8,128)(2,1)} fusion(bf16[2048,12,64]{0,2,1:T(8,128)(2,1)} %bitcast.294, f32[12,512,2048]{2,1,0:T(8,128)} %get-tuple-element.163, f32[12,512]{1,0:T(8,128)S(1)} %log_add_fusion, pred[512,2048]{1,0:T(8,128)(4,1)S(1)} %broadcast_compare_fusion), kind=kOutput, calls=%fused_computation.122 | convolution fusion | flops 1661337600 | bytes 55336960 | tf_op jit(solution)/shard_map/rhqk,rkhd->rqhd/dot_general | solution.py:110
  122.6 22.7 %fusion = (f32[12,512]{1,0:T(8,128)S(1)}, f32[12,512,2048]{2,1,0:T(8,128)}) fusion(pred[512,2048]{1,0:T(8,128)(4,1)S(1)} %broadcast_compare_fusion.1, bf16[512,12,64]{0,2,1:T(8,128)(2,1)S(1)} %bitcast.300, bf16[2048,12,64]{0,2,1:T(8,128)(2,1)} %bitcast.289), kind=kOutput, calls=%fused_computation.10 | convolution fusion | flops 1648355328 | bytes 55336960 | tf_op jit(solution)/shard_map/rqhd,rkhd->rhqk/dot_general | solution.py:48
  149.7 21.9 %exponential_reduce_fusion.1 = f32[12,512]{1,0:T(8,128)S(1)} fusion(f32[12,512,2048]{2,1,0:T(8,128)} %get-tuple-element.159, f32[12,512]{1,0:T(8,128)S(1)} %get-tuple-element.158, pred[512,2048]{1,0:T(8,128)(4,1)S(1)} %broadcast_compare_fusion.1), kind=kLoop, calls=%fused_computation.8 | loop fusion | flops 50325504 | bytes 51429376 | tf_op jit(solution)/shard_map/reduce_sum | solution.py:107
  176.3 20.3 %convolution_convert_fusion.1 = bf16[12,64,512]{2,1,0:T(8,128)(2,1)S(1)} fusion(bf16[2048,12,64]{0,2,1:T(8,128)(2,1)} %bitcast.296, f32[12,512,2048]{2,1,0:T(8,128)} %get-tuple-element.159, f32[12,512]{1,0:T(8,128)S(1)} %log_add_fusion.1, pred[512,2048]{1,0:T(8,128)(4,1)S(1)} %broadcast_compare_fusion.1), kind=kOutput, calls=%fused_computation.123 | convolution fusion | flops 1661337600 | bytes 55336960 | tf_op jit(solution)/shard_map/rhqk,rkhd->rqhd/dot_general | solution.py:110
  204.2 34.4 %multiply_convert_fusion.3 = (bf16[512,3072]{1,0:T(8,128)(2,1)S(1)}, f32[512,3072]{1,0:T(8,128)}, bf16[512,3072]{1,0:T(8,128)(2,1)S(1)}, f32[512,3072]{1,0:T(8,128)}, f32[512,3072]{1,0:T(8,128)}) fusion(f32[3072]{0:T(1024)S(1)} %copy-done.100, f32[512,3072]{1,0:T(8,128)S(1)} %fusion.136, bf16[768,3072]{1,0:T(8,128)(2,1)S(1)} %bitcast.325, ...), kind=kOutput, calls=%fused_computation.36 | convolution fusion | flops 2625503232 | bytes 37771264 | tf_op jit(solution)/shard_map/rtd,de->rte/dot_general | solution.py:27
  308.5 23.2 %fusion.112 = f32[12,64,2048]{2,1,0:T(8,128)} fusion(bf16[512,12,64]{0,2,1:T(8,128)(2,1)S(1)} %bitcast.310, f32[12,512,2048]{2,1,0:T(8,128)} %get-tuple-element.159, f32[12,512]{1,0:T(8,128)S(1)} %copy-done.58, pred[512,2048]{1,0:T(8,128)(4,1)S(1)} %copy-done.5), kind=kOutput, calls=%fused_computation.209 | convolution fusion | flops 1660944384 | bytes 58482688 | tf_op jit(solution)/shard_map/rhqk,rqhd->rkhd/dot_general | solution.py:167
  338.8 26.2 %fusion.109 = f32[12,64,2048]{2,1,0:T(8,128)} fusion(bf16[512,12,64]{0,2,1:T(8,128)(2,1)S(1)} %bitcast.308, f32[12,512,2048]{2,1,0:T(8,128)} %get-tuple-element.163, f32[12,512]{1,0:T(8,128)S(1)} %copy-done.56, pred[512,2048]{1,0:T(8,128)(4,1)S(1)} %copy-done.3), kind=kOutput, calls=%fused_computation.208 | convolution fusion | flops 1660944384 | bytes 58482688 | tf_op jit(solution)/shard_map/rhqk,rqhd->rkhd/dot_general | solution.py:167
  366.2 39.2 %multiply_reduce_fusion.1 = (f32[12,512]{1,0:T(8,128)S(1)}, f32[12,512,2048]{2,1,0:T(8,128)}) fusion(f32[12,512,2048]{2,1,0:T(8,128)} %get-tuple-element.159, f32[12,512]{1,0:T(8,128)S(1)} %copy-done.58, pred[512,2048]{1,0:T(8,128)(4,1)S(1)} %copy-done.5, bf16[512,12,64]{0,2,1:T(8,128)(2,1)S(1)} %bitcast.311, bf16[2048,12,64]{0,2,1:T(8,128)(2,1)} %bitcast.297), kind=kOutput, calls=%fused_computation.3 | convolution fusion | flops 1673521152 | bytes 105693184 | tf_op jit(solution)/shard_map/rqhd,rkhd->rhqk/dot_general | solution.py:151
  405.4 42.2 %multiply_convert_fusion.1 = bf16[12,512,2048]{2,1,0:T(8,128)(2,1)} fusion(f32[12,512,2048]{2,1,0:T(8,128)} %get-tuple-element.176, f32[12,512,2048]{2,1,0:T(8,128)} %get-tuple-element.159, f32[12,512]{1,0:T(8,128)S(1)} %get-tuple-element.175, f32[12,512]{1,0:T(8,128)S(1)} %copy-done.58, pred[512,2048]{1,0:T(8,128)(4,1)S(1)} %copy-done.5), kind=kLoop, calls=%fused_computation.2 | loop fusion | flops 75497472 | bytes 126926848 | tf_op jit(solution)/shard_map/convert_element_type | solution.py:154
  447.5 15.4 %convolution_multiply_fusion.1 = f32[12,64,2048]{2,1,0:T(8,128)} fusion(bf16[512,12,64]{0,2,1:T(8,128)(2,1)S(1)} %bitcast.301, bf16[12,512,2048]{2,1,0:T(8,128)(2,1)} %multiply_convert_fusion.1), kind=kOutput, calls=%fused_computation.53 | convolution fusion | flops 1612185600 | bytes 32243712 | tf_op jit(solution)/shard_map/rhqk,rqhd->rkhd/dot_general | solution.py:163
  464.1 38.3 %multiply_reduce_fusion = (f32[12,512]{1,0:T(8,128)S(1)}, f32[12,512,2048]{2,1,0:T(8,128)}) fusion(f32[12,512,2048]{2,1,0:T(8,128)} %get-tuple-element.163, f32[12,512]{1,0:T(8,128)S(1)} %copy-done.56, pred[512,2048]{1,0:T(8,128)(4,1)S(1)} %copy-done.3, bf16[512,12,64]{0,2,1:T(8,128)(2,1)S(1)} %bitcast.309, bf16[2048,12,64]{0,2,1:T(8,128)(2,1)} %bitcast.295), kind=kOutput, calls=%fused_computation.1 | convolution fusion | flops 1673521152 | bytes 105693184 | tf_op jit(solution)/shard_map/rqhd,rkhd->rhqk/dot_general | solution.py:151
  502.5 40.6 %multiply_convert_fusion = bf16[12,512,2048]{2,1,0:T(8,128)(2,1)} fusion(f32[12,512,2048]{2,1,0:T(8,128)} %get-tuple-element.174, f32[12,512,2048]{2,1,0:T(8,128)} %get-tuple-element.163, f32[12,512]{1,0:T(8,128)S(1)} %get-tuple-element.173, f32[12,512]{1,0:T(8,128)S(1)} %copy-done.56, pred[512,2048]{1,0:T(8,128)(4,1)S(1)} %copy-done.3), kind=kLoop, calls=%fused_computation | loop fusion | flops 75497472 | bytes 126926848 | tf_op jit(solution)/shard_map/convert_element_type | solution.py:154
  543.1 15.2 %convolution_multiply_fusion = f32[12,64,2048]{2,1,0:T(8,128)} fusion(bf16[512,12,64]{0,2,1:T(8,128)(2,1)S(1)} %bitcast.299, bf16[12,512,2048]{2,1,0:T(8,128)(2,1)} %multiply_convert_fusion), kind=kOutput, calls=%fused_computation.52 | convolution fusion | flops 1612185600 | bytes 32243712 | tf_op jit(solution)/shard_map/rhqk,rqhd->rkhd/dot_general | solution.py:163
  558.4 15.5 %convert_reduce_fusion.8 = (f32[12,64]{1,0:T(8,128)S(1)}, bf16[12,64,512]{2,1,0:T(8,128)(2,1)S(1)}) fusion(bf16[2048,12,64]{0,2,1:T(8,128)(2,1)} %bitcast.288, bf16[12,512,2048]{2,1,0:T(8,128)(2,1)} %multiply_convert_fusion), kind=kOutput, calls=%fused_computation.98 | convolution fusion | flops 1612184832 | bytes 29101056 | tf_op jit(solution)/shard_map/rhqk,rkhd->rqhd/dot_general | solution.py:158
  573.9 14.5 convert_reduce_fusion.9
  665.6 464.7 %all-reduce.10 = (bf16[9216]{0:T(1024)(128)(2,1)}, bf16[589824]{0:T(1024)(128)(2,1)}, bf16[589824]{0:T(1024)(128)(2,1)}, bf16[589824]{0:T(1024)(128)(2,1)}, bf16...) all-reduce(f32[9216]{0:T(1024)S(1)} %constant_dynamic-update-slice_, ...), channel_id=11, replica_groups=mesh['dp'=8,'seq'=4] {'dp','seq'}, use_global_device_ids=true, to_apply=%region_49.50.clone | all-reduce | flops 7087104 | bytes 42522624
  1147.9 37.4 %all-reduce = bf16[9216]{0:T(1024)(128)(2,1)S(1)} all-reduce(bf16[9216]{0:T(1024)(128)(2,1)S(1)} %dynamic-update-slice), channel_id=1, replica_groups=mesh['dp'=8,'seq'=4] {'dp','seq'}, use_global_device_ids=true, to_apply=%add | all-reduce | flops 9216 | bytes 36864
  1200.2 39.9 %all-gather.17.cloned.1.call-done = bf16[589824]{0:T(1024)(128)(2,1)} async-done(((bf16[18432]{0:T(1024)(128)(2,1)}), bf16[589824]{0:T(1024)(128)(2,1)}) %all-gather.17.cloned.1.call-update) | async-done | bytes 1179664 | tf_op jit(solution)/shard_map/all_gather | solution.py:230
  1243.4 52.6 %all-gather.19.cloned.1.call-done = bf16[589824]{0:T(1024)(128)(2,1)} async-done(((bf16[18432]{0:T(1024)(128)(2,1)}), bf16[589824]{0:T(1024)(128)(2,1)}) %all-gather.19.cloned.1.call-update) | async-done | bytes 1179664 | tf_op jit(solution)/shard_map/all_gather | solution.py:233
  1299.3 52.4 %all-gather.21.cloned.1.call-done = bf16[589824]{0:T(1024)(128)(2,1)} async-done(((bf16[18432]{0:T(1024)(128)(2,1)}), bf16[589824]{0:T(1024)(128)(2,1)}) %all-gather.21.cloned.1.call-update) | async-done | bytes 1179664 | tf_op jit(solution)/shard_map/all_gather | solution.py:236
  1355.0 62.7 %all-gather.23.cloned.1.call-done = bf16[2359296]{0:T(1024)(128)(2,1)} async-done(((bf16[73728]{0:T(1024)(128)(2,1)}), bf16[2359296]{0:T(1024)(128)(2,1)}) %all-gather.23.cloned.1.call-update) | async-done | bytes 4718608 | tf_op jit(solution)/shard_map/all_gather | solution.py:239
  1426.5 56.5 %all-gather.25.cloned.1.call-done = bf16[2359296]{0:T(1024)(128)(2,1)} async-done(((bf16[73728]{0:T(1024)(128)(2,1)}), bf16[2359296]{0:T(1024)(128)(2,1)}) %all-gather.25.cloned.1.call-update) | async-done | bytes 4718608 | tf_op jit(solution)/shard_map/all_gather | solution.py:242
  (400 shorter events, 282.1 us)
Async XLA Ops:
  7.2 138.1 %copy-start = (bf16[768,768]{1,0:T(8,128)(2,1)S(1)}, bf16[768,768]{1,0:T(8,128)(2,1)}, u32[]{:S(2)}) copy-start(bf16[768,768]{1,0:T(8,128)(2,1)} %param.26) | copy-start | bytes 3538948
  7.2 34.8 %all-gather.33.cloned.1.call-start = ((), (), s32[]{:S(2)}) async-start(), calls=%async_computation.17 | async-start | bytes 3932160 | tf_op jit(solution)/shard_map/all_gather | solution.py:99
  10.6 80.8 %all-gather.31.cloned.1.call-start = ((), (), s32[]{:S(2)}) async-start(), calls=%async_computation.16 | async-start | bytes 3932160 | tf_op jit(solution)/shard_map/all_gather | solution.py:100
  13.6 104.1 %all-gather.29.cloned.1.call-start = ((), (), s32[]{:S(2)}) async-start(), calls=%async_computation.15 | async-start | bytes 3932160 | tf_op jit(solution)/shard_map/all_gather | solution.py:99
  16.7 154.9 %all-gather.27.cloned.1.call-start = ((), (), s32[]{:S(2)}) async-start(), calls=%async_computation.14 | async-start | bytes 3932160 | tf_op jit(solution)/shard_map/all_gather | solution.py:100
  19.7 619.8 %reduce-scatter.7.cloned.1.call-start = ((), (), s32[]{:S(2)}) async-start(), calls=%async_computation.5 | async-start | bytes 7864320 | tf_op jit(solution)/shard_map/reduce_scatter | solution.py:173
  29.7 66.4 %copy-start.2 = (pred[512,2048]{1,0:T(8,128)(4,1)}, pred[512,2048]{1,0:T(8,128)(4,1)S(1)}, u32[]{:S(2)}) copy-start(pred[512,2048]{1,0:T(8,128)(4,1)S(1)} %broadcast_compare_fusion) | copy-start | bytes 3145732
  30.4 145.9 %copy-start.4 = (pred[512,2048]{1,0:T(8,128)(4,1)}, pred[512,2048]{1,0:T(8,128)(4,1)S(1)}, u32[]{:S(2)}) copy-start(pred[512,2048]{1,0:T(8,128)(4,1)S(1)} %broadcast_compare_fusion.1) | copy-start | bytes 3145732
  147.6 152.6 %copy-start.66 = (f32[512]{0:T(512)}, f32[512]{0:T(512)S(1)}, u32[]{:S(2)}) copy-start(f32[512]{0:T(512)S(1)} %broadcast_multiply_fusion.1) | copy-start | bytes 6148
  149.1 151.2 %copy-start.68 = (f32[512]{0:T(512)}, f32[512]{0:T(512)S(1)}, u32[]{:S(2)}) copy-start(f32[512]{0:T(512)S(1)} %fusion.117) | copy-start | bytes 6148
  197.7 102.6 %copy-start.70 = (f32[512]{0:T(512)}, f32[512]{0:T(512)S(1)}, u32[]{:S(2)}) copy-start(f32[512]{0:T(512)S(1)} %broadcast_multiply_fusion.3) | copy-start | bytes 6148
  198.4 101.9 %copy-start.84 = (f32[512]{0:T(512)}, f32[512]{0:T(512)S(1)}, u32[]{:S(2)}) copy-start(f32[512]{0:T(512)S(1)} %fusion.115) | copy-start | bytes 6148
  331.7 309.4 %reduce-scatter.11.cloned.1.call-start = ((), (), s32[]{:S(2)}) async-start(), calls=%async_computation.7 | async-start | bytes 7864320 | tf_op jit(solution)/shard_map/reduce_scatter | solution.py:173
  365.0 277.9 %reduce-scatter.5.cloned.1.call-start = ((), (), s32[]{:S(2)}) async-start(), calls=%async_computation.4 | async-start | bytes 7864320 | tf_op jit(solution)/shard_map/reduce_scatter | solution.py:172
  463.0 183.6 %reduce-scatter.9.cloned.1.call-start = ((), (), s32[]{:S(2)}) async-start(), calls=%async_computation.6 | async-start | bytes 7864320 | tf_op jit(solution)/shard_map/reduce_scatter | solution.py:172
  558.3 638.5 %all-gather.15.cloned.1.call-start = ((), (), s32[]{:S(2)}) async-start(), calls=%async_computation.8 | async-start | bytes 1216512 | tf_op jit(solution)/shard_map/all_gather | solution.py:227
  665.6 474.2 %copy-start.59 = (f32[2,15,768]{2,1,0:T(8,128)S(1)}, f32[2,15,768]{2,1,0:T(8,128)}, u32[]{:S(2)}) copy-start(f32[2,15,768]{2,1,0:T(8,128)} %get-tuple-element.157) | copy-start | bytes 276484
  665.6 474.9 %copy-start.42 = (bf16[1,512,768]{2,1,0:T(8,128)(2,1)S(1)}, bf16[1,512,768]{2,1,0:T(8,128)(2,1)}, u32[]{:S(2)}) copy-start(bf16[1,512,768]{2,1,0:T(8,128)(2,1)} %get-tuple-element.130) | copy-start | bytes 2359300
  1131.8 108.2 %all-gather.17.cloned.1.call-start = ((), (), s32[]{:S(2)}) async-start(), calls=%async_computation.9 | async-start | bytes 1216512 | tf_op jit(solution)/shard_map/all_gather | solution.py:230
  1133.3 162.7 %all-gather.19.cloned.1.call-start = ((), (), s32[]{:S(2)}) async-start(), calls=%async_computation.10 | async-start | bytes 1216512 | tf_op jit(solution)/shard_map/all_gather | solution.py:233
  1134.7 217.0 %all-gather.21.cloned.1.call-start = ((), (), s32[]{:S(2)}) async-start(), calls=%async_computation.11 | async-start | bytes 1216512 | tf_op jit(solution)/shard_map/all_gather | solution.py:236
  1136.2 281.6 %all-gather.23.cloned.1.call-start = ((), (), s32[]{:S(2)}) async-start(), calls=%async_computation.12 | async-start | bytes 4866048 | tf_op jit(solution)/shard_map/all_gather | solution.py:239
  1137.8 345.2 %all-gather.25.cloned.1.call-start = ((), (), s32[]{:S(2)}) async-start(), calls=%async_computation.13 | async-start | bytes 4866048 | tf_op jit(solution)/shard_map/all_gather | solution.py:242
  1145.0 45.7 %copy-start.77 = (f32[512]{0:T(512)S(1)}, f32[512]{0:T(512)}, u32[]{:S(2)}) copy-start(f32[512]{0:T(512)} %copy-done.76) | copy-start | bytes 6148
  (105 other events, 794.4 us)
Sparse Core Ops, SparseCore 0:
  10.7 31.2 all-gather.32
  44.1 28.5 all-gather.30
  74.9 28.5 all-gather.28
  105.4 28.5 all-gather.26
  331.9 59.2 reduce-scatter.6
  393.7 58.3 reduce-scatter.10
  463.1 59.4 reduce-scatter.4
  558.4 59.7 reduce-scatter.8
  1131.9 52.3 all-gather.14
  1187.0 52.9 all-gather.16
  1242.9 52.9 all-gather.18
  1298.7 52.9 all-gather.20
  1355.1 62.5 all-gather.22
  1420.5 62.4 all-gather.24
where the time goes:
time: 1510 us; the launch traced here: 1500 us
  blocking collectives  513 us (34%)
  matrix products  429 us (28%)
  waiting for transfers between devices  276 us (18%)
  other arithmetic  149 us (10%)
  local copies, waits for them, and re-layouts  116 us (8%)
  between operations  16 us (1%)
    unnamed x2, blocking collectives  502 us
    convert_element_type x2, other arithmetic, local(): (soft * (d_soft - jnp.sum(soft * d_soft, axis=3, keepdims=True))).astype(...  82.8 us
    dot_general x2, matrix products, local(): jnp.einsum('rqhd,rkhd->rhqk', d_attended, value_heads, preferred_element_...  77.5 us
    dot_general x12, matrix products, project(): jnp.einsum('rtd,de->rte', activations, weight, preferred_element_type=jnp...  64.9 us
    all_gather x1, waiting for transfers between devices, local(): lax.all_gather(up_part.astype(jnp.bfloat16), ('dp', 'seq'), axis=0, tiled...  62.7 us
    all_gather x1, waiting for transfers between devices, local(): lax.all_gather(down_part.astype(jnp.bfloat16), ('dp', 'seq'), axis=0, til...  56.5 us
    all_gather x1, waiting for transfers between devices, local(): lax.all_gather(value_part.astype(jnp.bfloat16), ('dp', 'seq'), axis=0, ti...  52.6 us
    all_gather x1, waiting for transfers between devices, local(): lax.all_gather(out_part.astype(jnp.bfloat16), ('dp', 'seq'), axis=0, tile...  52.4 us
  transfers between devices with their start and end apart: 14, of which 6 were waited for; matrix products, arithmetic and copies ran while one was open for 34% of the time, Pallas kernels for 0%

commit v1 on v0

v1 whole, which is shorter than its diff:
```python
import functools

import jax
import jax.numpy as jnp
from jax import lax
from jax.experimental import pallas as pl
from jax.experimental.pallas import tpu as pltpu
from jax.sharding import PartitionSpec as P

HD = 64
NSENT = 15
SLOTS = 16
EPS = 1e-06
HIGH = lax.Precision.HIGHEST
PAIR = 2 * HD
QB = 128
KB = 256
MASKED = -1e30
BF16 = jnp.bfloat16
F32 = jnp.float32


def swap(value, axis, bit):
    size = lax.axis_size(axis)
    return lax.ppermute(value, axis, [(i, i ^ bit) for i in range(size)])


def bit_of(axis, bit):
    return (lax.axis_index(axis) // bit) % 2


def dot(left, right, contract):
    return lax.dot_general(left, right, (contract, ((), ())), preferred_element_type=F32)


def qkv_kernel(place_ref, a_ref, b_ref, c_ref, d_ref, weight_ref, bias_ref, scale_ref, x_ref, out_ref):
    step = pl.program_id(0)
    for slot, source in enumerate((a_ref, b_ref, c_ref, d_ref)):

        @pl.when(step == slot)
        def _(source=source):
            x_ref[...] = source[...]
            total = dot(source[...], weight_ref[...], ((1,), (0,)))
            out_ref[...] = ((total + bias_ref[...]) * scale_ref[...]).astype(BF16)


def qkv(places, chunks, weight, bias, scale):
    length, width = chunks[0].shape
    columns = weight.shape[1]
    whole = lambda i, places: (0, 0)
    placed = lambda i, places: (places[i], 0)
    return pl.pallas_call(
        qkv_kernel,
        grid_spec=pltpu.PrefetchScalarGridSpec(
            num_scalar_prefetch=1,
            grid=(4,),
            in_specs=[pl.BlockSpec((length, width), whole)] * 4
            + [
                pl.BlockSpec((width, columns), whole),
                pl.BlockSpec((1, columns), whole),
                pl.BlockSpec((1, columns), whole),
            ],
            out_specs=[
                pl.BlockSpec((length, width), placed),
                pl.BlockSpec((length, columns), placed),
            ],
        ),
        out_shape=[
            jax.ShapeDtypeStruct((4 * length, width), BF16),
            jax.ShapeDtypeStruct((4 * length, columns), BF16),
        ],
        cost_estimate=pl.CostEstimate(
            flops=8 * length * width * columns, bytes_accessed=20 * length * width, transcendentals=0
        ),
    )(places, *chunks, weight, bias, scale)


def halves(block):
    lane = lax.broadcasted_iota(jnp.int32, block.shape, 1)
    zero = jnp.zeros_like(block)
    return jnp.where(lane < HD, block, zero), jnp.where(lane < HD, zero, block)


def stack_heads(block, feature=None):
    first, second = halves(block)
    if feature is not None:
        first = jnp.concatenate([first, feature], axis=1)
        second = jnp.concatenate([second, feature], axis=1)
    return jnp.concatenate([first, second], axis=0)


def merge_heads(stacked):
    first, second = stacked[:QB], stacked[QB:]
    lane = lax.broadcasted_iota(jnp.int32, first.shape, 1)
    return jnp.where(lane < HD, first, second)


def attend_kernel(start_ref, count_ref, q_ref, k_ref, v_ref, qf_ref, kf_ref, out_ref, lse_ref, score_ref, acc_ref):
    @pl.loop(0, q_ref.shape[0] // QB)
    def _(block):
        rows = pl.ds(pl.multiple_of(block * QB, QB), QB)
        start = start_ref[block] * QB
        count = count_ref[block]
        stacked = stack_heads(q_ref[rows, :], qf_ref[rows, :])

        def scores(j, top):
            keys = pl.ds(pl.multiple_of(start + j * KB, QB), KB)
            side = jnp.concatenate([k_ref[keys, :], kf_ref[keys, :]], axis=1)
            score = dot(side, stacked, ((1,), (1,)))
            score_ref[pl.ds(pl.multiple_of(j * KB, KB), KB), :] = score
            return jnp.maximum(top, jnp.max(score.reshape(KB // 8, 8, 2 * QB), axis=0))

        top = lax.fori_loop(0, count, scores, jnp.full((8, 2 * QB), -jnp.inf, F32))
        top = jnp.max(top, axis=0, keepdims=True)
        acc_ref[...] = jnp.zeros_like(acc_ref)

        def weigh(j, total):
            keys = pl.ds(pl.multiple_of(start + j * KB, QB), KB)
            soft = jnp.exp(score_ref[pl.ds(pl.multiple_of(j * KB, KB), KB), :] - top)
            value = v_ref[keys, :]
            side = jnp.concatenate([value, jnp.ones_like(value)], axis=1)
            acc_ref[...] += dot(soft.astype(BF16), side, ((0,), (0,)))
            return total + jnp.sum(soft.reshape(KB // 8, 8, 2 * QB), axis=0)

        total = lax.fori_loop(0, count, weigh, jnp.zeros((8, 2 * QB), F32))
        total = jnp.sum(total, axis=0, keepdims=True)
        lse_ref[0, pl.ds(block, 1), :] = top + jnp.log(total)
        acc = acc_ref[...]
        out_ref[rows, :] = merge_heads(acc[:, :PAIR] / acc[:, PAIR:]).astype(BF16)


def attend(starts, counts, packed, query_feature, key_feature):
    length = packed.shape[0]
    pairs = packed.shape[1] // (3 * PAIR)
    column = lambda offset: pl.BlockSpec((length, PAIR), lambda g, s, c: (0, g + offset * pairs))
    feature = pl.BlockSpec((length, PAIR), lambda g, s, c: (0, 0))
    return pl.pallas_call(
        attend_kernel,
        grid_spec=pltpu.PrefetchScalarGridSpec(
            num_scalar_prefetch=2,
            grid=(pairs,),
            in_specs=[column(0), column(1), column(2), feature, feature],
            out_specs=[
                pl.BlockSpec((length, PAIR), lambda g, s, c: (0, g)),
                pl.BlockSpec((1, length // QB, 2 * QB), lambda g, s, c: (g, 0, 0)),
            ],
            scratch_shapes=[pltpu.VMEM((length, 2 * QB), F32), pltpu.VMEM((2 * QB, 2 * PAIR), F32)],
        ),
        out_shape=[
            jax.ShapeDtypeStruct((length, pairs * PAIR), BF16),
            jax.ShapeDtypeStruct((pairs, length // QB, 2 * QB), F32),
        ],
        compiler_params=pltpu.CompilerParams(vmem_limit_bytes=48 << 20),
        cost_estimate=pl.CostEstimate(
            flops=16 * length * length * PAIR, bytes_accessed=12 * length * PAIR, transcendentals=length * length
        ),
    )(starts, counts, packed, packed, packed, query_feature, key_feature)


def attend_back_kernel(
    start_ref, count_ref, q_ref, k_ref, v_ref, o_ref, do_ref, lse_ref, qf_ref, kf_ref,
    dq_ref, dk_ref, dv_ref, dq_acc, dk_acc, dv_acc,
):
    dk_acc[...] = jnp.zeros_like(dk_acc)
    dv_acc[...] = jnp.zeros_like(dv_acc)

    @pl.loop(0, q_ref.shape[0] // QB)
    def _(block):
        rows = pl.ds(pl.multiple_of(block * QB, QB), QB)
        start = start_ref[block] * QB
        count = count_ref[block]
        query = q_ref[rows, :]
        stacked = stack_heads(query, qf_ref[rows, :])
        queries = stack_heads(query)
        upstream = do_ref[rows, :]
        ups = stack_heads(upstream)
        product = (upstream.astype(F32) * o_ref[rows, :].astype(F32)).T
        delta = jnp.concatenate(
            [jnp.sum(product[:HD], axis=0, keepdims=True), jnp.sum(product[HD:], axis=0, keepdims=True)], axis=1
        )
        lse = lse_ref[0, pl.ds(block, 1), :]
        dq_acc[...] = jnp.zeros_like(dq_acc)

        @pl.loop(0, count)
        def _(j):
            keys = pl.ds(pl.multiple_of(start + j * KB, QB), KB)
            key = k_ref[keys, :]
            score = dot(jnp.concatenate([key, kf_ref[keys, :]], axis=1), stacked, ((1,), (1,)))
            soft = jnp.exp(score - lse)
            d_soft = dot(v_ref[keys, :], ups, ((1,), (1,)))
            d_score = (soft * (d_soft - delta)).astype(BF16)
            dv_acc[keys, :] += dot(soft.astype(BF16), ups, ((1,), (0,)))
            dk_acc[keys, :] += dot(d_score, queries, ((1,), (0,)))
            dq_acc[...] += dot(d_score, key, ((0,), (0,)))

        dq_ref[rows, :] = (merge_heads(dq_acc[...]) * 0.125).astype(BF16)

    dk_ref[...] = dk_acc[...].astype(BF16)
    dv_ref[...] = dv_acc[...].astype(BF16)


def attend_back(starts, counts, packed, attended, upstream, lse, query_feature, key_feature):
    length = packed.shape[0]
    pairs = packed.shape[1] // (3 * PAIR)
    column = lambda offset: pl.BlockSpec((length, PAIR), lambda g, s, c: (0, g + offset * pairs))
    feature = pl.BlockSpec((length, PAIR), lambda g, s, c: (0, 0))
    return pl.pallas_call(
        attend_back_kernel,
        grid_spec=pltpu.PrefetchScalarGridSpec(
            num_scalar_prefetch=2,
            grid=(pairs,),
            in_specs=[column(0), column(1), column(2), column(0), column(0)]
            + [pl.BlockSpec((1, length // QB, 2 * QB), lambda g, s, c: (g, 0, 0)), feature, feature],
            out_specs=[column(0)] * 3,
            scratch_shapes=[
                pltpu.VMEM((2 * QB, PAIR), F32),
                pltpu.VMEM((length, PAIR), F32),
                pltpu.VMEM((length, PAIR), F32),
            ],
        ),
        out_shape=[jax.ShapeDtypeStruct((length, pairs * PAIR), BF16)] * 3,
        compiler_params=pltpu.CompilerParams(vmem_limit_bytes=48 << 20),
        cost_estimate=pl.CostEstimate(
            flops=40 * length * length * PAIR, bytes_accessed=20 * length * PAIR, transcendentals=length * length
        ),
    )(starts, counts, packed, packed, packed, attended, upstream, lse, query_feature, key_feature)


def reduce_step(value, axis, bit):
    half = value.shape[0] // 2
    mine = bit_of(axis, bit)
    keep = lax.dynamic_slice_in_dim(value, mine * half, half, 0)
    send = lax.dynamic_slice_in_dim(value, (1 - mine) * half, half, 0)
    got = swap(send, axis, bit)
    return (keep.astype(F32) + got.astype(F32)).astype(BF16)


def gather_step(value, axis, bit):
    got = swap(value, axis, bit)
    first = bit_of(axis, bit) == 0
    return jnp.concatenate([jnp.where(first, value, got), jnp.where(first, got, value)], axis=0)


def all_reduce(value, order):
    for axis, bit in order:
        value = reduce_step(value, axis, bit)
    for axis, bit in reversed(order):
        value = gather_step(value, axis, bit)
    return value


def sum_all(value, order):
    for axis, bit in order:
        value = value + swap(value, axis, bit)
    return value


def layer_norm(hidden, norm_gain, norm_shift):
    centred = hidden - jnp.mean(hidden, axis=-1, keepdims=True)
    spread = jnp.mean(centred * centred, axis=-1, keepdims=True)
    return centred * lax.rsqrt(spread + EPS) * norm_gain + norm_shift


def gelu_exact(values):
    return jax.nn.gelu(values, approximate=False)


def local(
    hidden_in,
    seg_lengths,
    query_weight,
    query_bias,
    key_weight,
    value_weight,
    value_bias,
    out_weight,
    out_bias,
    first_gain,
    first_shift,
    up_weight,
    up_bias,
    down_weight,
    down_bias,
    second_gain,
    second_shift,
    cot_out,
    cot_pool,
):
    _, chunk, width = hidden_in.shape
    length = 4 * chunk
    half = width // 2
    dp_bits = [1 << i for i in range((lax.axis_size("dp") - 1).bit_length())]
    dp_order = [("dp", b) for b in dp_bits]
    far, near = ("seq", 2), ("seq", 1)
    high, low = bit_of(*far), bit_of(*near)
    mine = lax.axis_index("seq")

    pick = lambda array, i: lax.dynamic_index_in_dim(array, i, 0, keepdims=False)
    own = pick(hidden_in, high)
    came = swap(pick(hidden_in, 1 - high), *far)
    own_there = swap(own, *near)
    came_there = swap(came, *near)
    cot_own = pick(cot_out, high)
    cot_came = swap(pick(cot_out, 1 - high), *far)

    lengths = pick(seg_lengths, high)
    ends = jnp.cumsum(lengths)
    begins = ends - lengths
    sizes = lengths[:NSENT].astype(F32)
    positions = jnp.arange(length, dtype=jnp.int32)
    member = (positions[:, None] >= begins[None, :]) & (positions[:, None] < ends[None, :])
    member = jnp.pad(member, ((0, 0), (0, PAIR - SLOTS)))
    query_feature = member.astype(BF16)
    key_feature = jnp.where(member, 0.0, MASKED).astype(BF16)
    block_first = jnp.arange(length // QB, dtype=jnp.int32) * QB
    block_last = block_first + QB - 1
    holds = lambda t: (t[:, None] >= begins[None, :]) & (t[:, None] < ends[None, :])
    lowest = jnp.sum(jnp.where(holds(block_first), begins[None, :], 0), axis=1)
    highest = jnp.sum(jnp.where(holds(block_last), ends[None, :], 0), axis=1)
    starts = lowest // QB
    stops = (highest + QB - 1) // QB
    counts = (stops - starts + 1) // (KB // QB)
    starts = jnp.minimum(starts, length // QB - counts * (KB // QB))

    take = lambda weight: lax.dynamic_slice_in_dim(weight, low * half, half, 1)
    packed_weight = jnp.concatenate([take(query_weight), take(key_weight), take(value_weight)], axis=1)
    vector = lambda bias: lax.dynamic_slice_in_dim(bias, low * half, half, 0)
    packed_bias = jnp.concatenate([vector(query_bias), jnp.zeros((half,), F32), vector(value_bias)])[None, :]
    scale = jnp.concatenate([jnp.full((half,), 0.125, F32), jnp.ones((2 * half,), F32)])[None, :]

    places = jnp.stack([mine, mine ^ 2, mine ^ 1, mine ^ 3]).astype(jnp.int32)
    row_input, packed = qkv(places, (own, came, own_there, came_there), packed_weight, packed_bias, scale)
    attended_heads, lse = attend(starts, counts, packed, query_feature, key_feature)

    def to_tokens(array):
        view = array.reshape(2, 2, chunk, half)
        keep = lax.dynamic_index_in_dim(view, low, 1, keepdims=False)
        send = lax.dynamic_index_in_dim(view, 1 - low, 1, keepdims=False)
        return keep.reshape(2 * chunk, half), swap(send.reshape(2 * chunk, half), *near)

    att_mine, att_other = to_tokens(attended_heads)
    out_mine = lax.dynamic_slice_in_dim(out_weight, low * half, half, 0)
    out_other = lax.dynamic_slice_in_dim(out_weight, (1 - low) * half, half, 0)

    by_place = lambda a, b: jnp.concatenate([jnp.where(high == 0, a, b), jnp.where(high == 0, b, a)], axis=0)
    inputs = by_place(own, came)
    cot = by_place(cot_own, cot_came)
    token_member = lax.dynamic_index_in_dim(member.reshape(2, 2, chunk, PAIR), low, 1, keepdims=False)
    token_member = token_member.reshape(2 * chunk, PAIR)[:, :NSENT].astype(F32)

    project = lambda a, w: dot(a, w, ((1,), (0,)))
    project_back = lambda a, w: dot(a, w, ((1,), (1,)))
    weight_grad = lambda a, g: dot(a, g, ((0,), (0,))).astype(BF16)
    column_sum = lambda g: jnp.sum(g.astype(F32), axis=0)

    first_sum = inputs.astype(F32) + project(att_mine, out_mine) + project(att_other, out_other) + out_bias
    normed, first_back = jax.vjp(layer_norm, first_sum, first_gain, first_shift)
    normed_low = normed.astype(BF16)
    pre_act = project(normed_low, up_weight) + up_bias
    activated, gelu_back = jax.vjp(gelu_exact, pre_act)
    activated_low = activated.astype(BF16)
    second_sum = normed + project(activated_low, down_weight) + down_bias
    final_norm, second_back = jax.vjp(layer_norm, second_sum, second_gain, second_shift)
    final_low = final_norm.astype(BF16)
    pool_part = lax.dot_general(
        token_member, final_norm, (((0,), (0,)), ((), ())), precision=HIGH, preferred_element_type=F32
    )
    pool_weights = pick(cot_pool, high) / sizes[:, None]
    upstream = cot.astype(F32) + jnp.dot(token_member, pool_weights, precision=HIGH, preferred_element_type=F32)
    d_second, d_gain_two, d_shift_two = second_back(upstream)
    d_branch = d_second.astype(BF16)
    d_down = weight_grad(activated_low, d_branch)
    (d_pre,) = gelu_back(project_back(d_branch, down_weight))
    d_pre_low = d_pre.astype(BF16)
    d_up = weight_grad(normed_low, d_pre_low)
    d_normed = d_second + project_back(d_pre_low, up_weight)
    d_first, d_gain_one, d_shift_one = first_back(d_normed)
    d_attn_out = d_first.astype(BF16)
    d_att_mine = project_back(d_attn_out, out_mine).astype(BF16)
    d_att_other = project_back(d_attn_out, out_other).astype(BF16)
    d_out_mine = dot(att_mine, d_attn_out, ((0,), (0,)))
    d_out_other = weight_grad(att_other, d_attn_out)

    d_att_came = swap(d_att_other, *near)
    pieces = (d_att_mine.reshape(2, 1, chunk, half), d_att_came.reshape(2, 1, chunk, half))
    d_attended = jnp.concatenate(
        [jnp.where(low == 0, pieces[0], pieces[1]), jnp.where(low == 0, pieces[1], pieces[0])], axis=1
    ).reshape(length, half)
    d_query, d_keys, d_values = attend_back(
        starts, counts, packed, attended_heads, d_attended, lse, query_feature, key_feature
    )
    d_packed = jnp.concatenate([d_query, d_keys, d_values], axis=1)
    d_hidden = project_back(d_packed, packed_weight).reshape(2, 2, chunk, width)
    d_hidden_keep = lax.dynamic_index_in_dim(d_hidden, low, 1, keepdims=False)
    d_hidden_send = lax.dynamic_index_in_dim(d_hidden, 1 - low, 1, keepdims=False)
    d_hidden_got = swap(d_hidden_send.astype(BF16), *near)
    d_inputs = d_first.reshape(2, chunk, width) + d_hidden_keep + d_hidden_got.astype(F32)
    d_packed_weight = weight_grad(row_input, d_packed)

    def to_rows(array):
        keep = pick(array, high)
        came = swap(pick(array, 1 - high), *far)
        return jnp.stack([jnp.where(high == 0, keep, came), jnp.where(high == 0, came, keep)])

    layer_out = to_rows(final_low.reshape(2, chunk, width))
    grad_own = pick(d_inputs, high)
    grad_came = swap(pick(d_inputs, 1 - high).astype(BF16), *far).astype(F32)
    grad_hidden = jnp.stack([jnp.where(high == 0, grad_own, grad_came), jnp.where(high == 0, grad_came, grad_own)])

    pool_row = (pool_part + swap(pool_part, *near)) / sizes[:, None]
    pool_far = swap(pool_row, *far)
    pooled = jnp.stack([jnp.where(high == 0, pool_row, pool_far), jnp.where(high == 0, pool_far, pool_row)])

    order_a = [far] + dp_order
    order_b = dp_order + [far]

    def reduce_columns(value):
        middle = value.shape[1] // 2
        return jnp.concatenate(
            [all_reduce(value[:, :middle], order_a), all_reduce(value[:, middle:], order_b)], axis=1
        )

    grad_down = gather_step(reduce_columns(reduce_step(d_down, *near)), *near).astype(F32)
    grad_up = gather_step(reduce_columns(reduce_step(d_up, *near)), *near).astype(F32)
    d_out = (d_out_mine + swap(d_out_other, *near).astype(F32)).astype(BF16)
    grad_out = gather_step(reduce_columns(d_out), *near).astype(F32)
    packed_all = reduce_columns(d_packed_weight)
    packed_there = swap(packed_all, *near)
    side = lambda i: jnp.concatenate(
        [
            jnp.where(low == 0, packed_all[:, i * half : (i + 1) * half], packed_there[:, i * half : (i + 1) * half]),
            jnp.where(low == 0, packed_there[:, i * half : (i + 1) * half], packed_all[:, i * half : (i + 1) * half]),
        ],
        axis=1,
    ).astype(F32)

    spread = lambda part: jnp.where(
        low == 0, jnp.concatenate([part, jnp.zeros_like(part)]), jnp.concatenate([jnp.zeros_like(part), part])
    )
    small = jnp.concatenate(
        [
            spread(column_sum(d_query)),
            spread(column_sum(d_values)),
            column_sum(d_attn_out),
            d_gain_one,
            d_shift_one,
            column_sum(d_pre_low),
            column_sum(d_branch),
            d_gain_two,
            d_shift_two,
        ]
    )
    small = sum_all(small.reshape(-1, width), [near, far] + dp_order).reshape(-1)
    hidden_units = up_weight.shape[1]
    pieces, offset = [], 0
    for size in (width, width, width, width, width, hidden_units, width, width, width):
        pieces.append(small[offset : offset + size])
        offset += size
    return (
        layer_out,
        pooled,
        grad_hidden,
        side(0),
        pieces[0],
        side(1),
        side(2),
        pieces[1],
        grad_out,
        pieces[2],
        pieces[3],
        pieces[4],
        grad_up,
        pieces[5],
        grad_down,
        pieces[6],
        pieces[7],
        pieces[8],
    )


def solution(mesh):
    tokens, rows = P("dp", "seq", None), P("dp", None)
    pool = P("dp", None, None)
    return jax.shard_map(
        local,
        mesh=mesh,
        in_specs=(tokens, rows) + (P(),) * 15 + (tokens, pool),
        out_specs=(tokens, pool, tokens) + (P(),) * 15,
        check_vma=False,
    )
```

time: 1510 us -> 687 us (0.45)
  blocking collectives: 513 us -> 0 us
  matrix products: 429 us -> 103 us
  Pallas kernels: 0 us -> 192 us
  starting transfers between devices: 0.83 us -> 85.4 us
  waiting for transfers between devices: 276 us -> 192 us
  local copies, waits for them, and re-layouts: 116 us -> 32.3 us
  other arithmetic: 149 us -> 74.9 us
    unnamed x2 -> x0, blocking collectives: 502 us -> none
    dot_general x52 -> x16, matrix products: 429 us -> 103 us  [the longest x14 98.4 us: dot(): lax.dot_general(left, right, (contract, ((), ())), preferred_element_type...]
    all_gather x10 -> x0, waiting for transfers between devices: 276 us -> none  [the longest x1 62.7 us: local(): lax.all_gather(up_part.astype(jnp.bfloat16), ('dp', 'seq'), axis=0, tiled...]
    ppermute x0 -> x87, waiting for transfers between devices: none -> 192 us  [swap(): return lax.ppermute(value, axis, [(i, i ^ bit) for i in range(size)])]
    pallas_call x0 -> x3, Pallas kernels: none -> 192 us  [the longest x1 96.5 us: attend_back(): pl.pallas_call(attend_back_kernel, grid_spec=pltpu.PrefetchScalarGridSpec...]
    ppermute x0 -> x87, starting transfers between devices: none -> 85.4 us  [swap(): return lax.ppermute(value, axis, [(i, i ^ bit) for i in range(size)])]
    convert_element_type x3 -> x43, other arithmetic: 83.3 us -> 25.8 us  [the longest x34 9.76 us: reduce_step(): return (keep.astype(F32) + got.astype(F32)).astype(BF16)]
    reshape x11 -> x3, local copies, waits for them, and re-layouts: 54.6 us -> 0.1 us  [the longest x1 10.9 us: local(): down_flat = grad_totals[11].reshape(-1)]
  transfers between devices with their start and end apart: 14 -> 87, of which waited for: 6 -> 54; matrix products, arithmetic and copies ran while one was open for 34% -> 13% of each run, Pallas kernels for 0% -> 28%
where the time goes in v1:
time: 687 us; the launch traced here: 682 us
  waiting for transfers between devices  192 us (28%)
  Pallas kernels  192 us (28%)
  matrix products  103 us (15%)
  starting transfers between devices  85.4 us (12%)
  other arithmetic  74.9 us (11%)
  local copies, waits for them, and re-layouts  32.3 us (5%)
    ppermute x87, waiting for transfers between devices, swap(): return lax.ppermute(value, axis, [(i, i ^ bit) for i in range(size)])  192 us
    dot_general x14, matrix products, dot(): lax.dot_general(left, right, (contract, ((), ())), preferred_element_type...  98.4 us
    pallas_call x1, Pallas kernels, attend_back(): pl.pallas_call(attend_back_kernel, grid_spec=pltpu.PrefetchScalarGridSpec...  96.5 us
    ppermute x87, starting transfers between devices, swap(): return lax.ppermute(value, axis, [(i, i ^ bit) for i in range(size)])  85.4 us
    pallas_call x1, Pallas kernels, attend(): pl.pallas_call(attend_kernel, grid_spec=pltpu.PrefetchScalarGridSpec(num_...  84.8 us
    select_n x35, other arithmetic, gather_step(): jnp.where(first, value, got)  23.3 us
  transfers between devices with their start and end apart: 87, of which 54 were waited for; matrix products, arithmetic and copies ran while one was open for 13% of the time, Pallas kernels for 28%

profile of v1, /device:TPU:0, one launch (start us, length us, event | category | flops | bytes accessed | tf_op | source)
XLA Modules:
  0.0 682.0 jit_solution(17849642954559125967)
XLA Ops:
  13.6 10.8 %collective-permute-done.b_ref = bf16[512,768]{1,0:T(8,128)(2,1)S(1)} collective-permute-done((bf16[512,768]{1,0:T(8,128)(2,1)}, bf16[512,768]{1,0:T(8,128)(2,1)S(1)}, u32[]{:S(2)}, u32[]{:S(2)}) %collective-permute-start) | collective-permute-done | bytes 786464 | tf_op jit(solution)/shard_map/ppermute | solution.py:25
  30.5 10.1 %shard_map.322 = (bf16[2048,768]{1,0:T(8,128)(2,1)}, bf16[2048,1152]{1,0:T(8,128)(2,1)}) custom-call(s32[4]{0:T(128)} %pad_add_fusion.place_ref, bf16[512,768]{1,0:T(8,128)(2,1)} %get-tuple-element.114.a_ref, bf16[512,768]{1,0:T(8,128)(2,1)} %copy-done.12, bf16[512,768]{1,0:T(8,128)(2,1)} %collective-permute-done.1.c_ref, ...), custom_call_target="tpu_custom_call" | custom-call | flops 3623878656 | bytes 7864320 | tf_op jit(solution)/shard_map/pallas_call | solution.py:52
  40.6 84.8 %shard_map.323 = (bf16[2048,384]{1,0:T(8,128)(2,1)S(1)}, f32[3,16,256]{2,1,0:T(8,128)S(1)}) custom-call(s32[16]{0:T(128)S(1)} %get-tuple-element.115.start_ref, s32[16]{0:T(128)S(1)} %get-tuple-element.116.count_ref, bf16[2048,1152]{1,0:T(8,128)(2,1)} %get-tuple-element.25.q_ref.k_ref.v_ref, bf16[2048,1152]{1,0:T(8,128)(2,1)} %get-tuple-element.25.q_ref.k_ref.v_ref, ...), custom_call_target="tpu_custom_call" | custom-call | flops 8589934592 | bytes 3145728 | tf_op jit(solution)/shard_map/pallas_call | solution.py:137
  134.1 35.0 %multiply_convert_fusion = (bf16[1024,3072]{1,0:T(8,128)(2,1)S(1)}, f32[1024,3072]{1,0:T(8,128)}, f32[1024,3072]{1,0:T(8,128)}) fusion(f32[3072]{0:T(1024)S(1)} %copy-done.34, bf16[768,3072]{1,0:T(8,128)(2,1)S(1)} %bitcast.127, f32[1024,768]{1,0:T(8,128)S(1)} %get-tuple-element.221, f32[768]{0:T(1024)S(1)} %copy-done.36, f32[768]{0:T(1024)S(1)} %copy-done.30, ...), kind=kOutput, calls=%fused_computation.4 | convolution fusion | flops 5043388416 | bytes 39348224 | tf_op jit(solution)/shard_map/dot_general | solution.py:33
  169.3 5.4 fusion.58
  184.3 16.9 %convert_reduce_fusion = (f32[3072]{0:T(1024)S(1)}, bf16[1024,3072]{1,0:T(8,128)(2,1)}) fusion(f32[1024,3072]{1,0:T(8,128)} %get-tuple-element.112, bf16[1024,768]{1,0:T(8,128)(2,1)S(1)} %get-tuple-element.103, bf16[3072,768]{1,0:T(8,128)(2,1)} %param.32, f32[1024,3072]{1,0:T(8,128)} %get-tuple-element.222, f32[3072]{0:T(1024)S(1)} %copy-done.34), kind=kOutput, calls=%fused_computation.2 | convolution fusion | flops 4885312512 | bytes 37773312 | tf_op jit(solution)/shard_map/dot_general | solution.py:33
  201.2 11.0 %multiply_reduce_fusion.1 = (f32[768]{0:T(1024)S(1)}, f32[1024]{0:T(1024)S(1)}, f32[768]{0:T(1024)S(1)}, f32[1024,768]{1,0:T(8,128)S(1)}) fusion(f32[1024,768]{1,0:T(8,128)} %copy-done.2, f32[1024]{0:T(1024)S(1)} %fusion.42, f32[1024]{0:T(1024)S(1)} %broadcast_multiply_fusion.1, f32[768]{0:T(1024)S(1)} %copy-done.30, ...), kind=kOutput, calls=%fused_computation.33 | convolution fusion | flops 4839699456 | bytes 20472832 | tf_op jit(solution)/shard_map/dot_general | solution.py:33
  218.2 6.5 convolution_convert_fusion.1
  224.7 6.0 convolution_convert_fusion
  240.9 13.8 %collective-permute-done.6 = f32[15,768]{1,0:T(8,128)S(1)} collective-permute-done((f32[15,768]{1,0:T(8,128)S(1)}, f32[15,768]{1,0:T(8,128)S(1)}, u32[]{:S(2)}, u32[]{:S(2)}) %collective-permute-start.6) | collective-permute-done | bytes 46112 | tf_op jit(solution)/shard_map/ppermute | solution.py:25
  272.8 96.5 %shard_map.324 = (bf16[2048,384]{1,0:T(8,128)(2,1)S(1)}, bf16[2048,384]{1,0:T(8,128)(2,1)S(1)}, bf16[2048,384]{1,0:T(8,128)(2,1)S(1)}) custom-call(s32[16]{0:T(128)S(1)} %get-tuple-element.115.start_ref, s32[16]{0:T(128)S(1)} %get-tuple-element.116.count_ref, bf16[2048,1152]{1,0:T(8,128)(2,1)} %get-tuple-element.25.q_ref.k_ref.v_ref, ...), custom_call_target="tpu_custom_call" | custom-call | flops 21474836480 | bytes 5242880 | tf_op jit(solution)/shard_map/pallas_call | solution.py:207
  371.5 6.2 fusion.45
  377.7 5.6 convolution_convert_fusion.2
  457.6 6.1 collective-permute-done.11
  493.0 6.6 collective-permute-done.14
  503.8 5.1 collective-permute-done.15
  516.5 5.1 collective-permute-done.25
  542.4 12.6 %collective-permute-done.52 = bf16[192,1536]{1,0:T(8,128)(2,1)S(1)} collective-permute-done((bf16[192,1536]{1,0:T(8,128)(2,1)S(1)}, bf16[192,1536]{1,0:T(8,128)(2,1)S(1)}, u32[]{:S(2)}, u32[]{:S(2)}) %collective-permute-start.52) | collective-permute-done | bytes 589856 | tf_op jit(solution)/shard_map/ppermute | solution.py:25
  573.5 6.8 collective-permute-done.62
  619.3 7.3 %collective-permute-done.67 = bf16[192,1536]{1,0:T(8,128)(2,1)S(1)} collective-permute-done((bf16[192,1536]{1,0:T(8,128)(2,1)S(1)}, bf16[192,1536]{1,0:T(8,128)(2,1)S(1)}, u32[]{:S(2)}, u32[]{:S(2)}) %collective-permute-start.67) | collective-permute-done | bytes 589856 | tf_op jit(solution)/shard_map/ppermute | solution.py:25
  630.1 6.5 collective-permute-done.85
  636.7 7.8 %collective-permute-done.77 = bf16[768,384]{1,0:T(8,128)(2,1)S(1)} collective-permute-done((bf16[768,384]{1,0:T(8,128)(2,1)S(1)}, bf16[768,384]{1,0:T(8,128)(2,1)S(1)}, u32[]{:S(2)}, u32[]{:S(2)}) %collective-permute-start.77) | collective-permute-done | bytes 589856 | tf_op jit(solution)/shard_map/ppermute | solution.py:25
  652.6 10.3 %broadcast_select_fusion.3 = (bf16[384,3072]{1,0:T(8,128)(2,1)S(1)}, bf16[384,3072]{1,0:T(8,128)(2,1)S(1)}) fusion(bf16[384,3072]{1,0:T(8,128)(2,1)S(1)} %collective-permute-done.68, pred[]{:T(512)S(6)} %eq.138, bf16[192,1536]{1,0:T(8,128)(2,1)S(1)} %get-tuple-element.155, bf16[192,1536]{1,0:T(8,128)(2,1)S(1)} %get-tuple-element.154, ...), kind=kLoop, calls=%fused_computation.56 | loop fusion | flops 11796480 | bytes 9437185 | tf_op jit(solution)/shard_map/jit(_where)/select_n | solution.py:241
  667.9 9.4 %broadcast_select_fusion.1 = (bf16[1536,768]{1,0:T(8,128)(2,1)S(1)}, bf16[1536,768]{1,0:T(8,128)(2,1)S(1)}) fusion(bf16[1536,768]{1,0:T(8,128)(2,1)S(1)} %collective-permute-done.86, pred[]{:T(512)S(6)} %eq.138, bf16[768,384]{1,0:T(8,128)(2,1)S(1)} %get-tuple-element.151, bf16[768,384]{1,0:T(8,128)(2,1)S(1)} %get-tuple-element.150, ...), kind=kLoop, calls=%fused_computation.54 | loop fusion | flops 11796480 | bytes 9437185 | tf_op jit(solution)/shard_map/jit(_where)/select_n | solution.py:241
  (506 shorter events, 286.7 us)
Async XLA Ops:
  2.9 21.5 %collective-permute-start = (bf16[512,768]{1,0:T(8,128)(2,1)}, bf16[512,768]{1,0:T(8,128)(2,1)S(1)}, u32[]{:S(2)}, u32[]{:S(2)}) collective-permute-start(bf16[512,768]{1,0:T(8,128)(2,1)} %dynamic-slice_bitcast_fusion.2), channel_id=1, source_target_pairs={{0,2},{1,3},{2,0},{3,1},{4,6},{5,7},{6,4},{7,5},{8,10},{9,11},{10,... | collective-permute-start | bytes 2359304 | tf_op jit(solution)/shard_map/ppermute | solution.py:25
  7.9 119.4 %collective-permute-start.7 = (bf16[512,768]{1,0:T(8,128)(2,1)}, bf16[512,768]{1,0:T(8,128)(2,1)}, u32[]{:S(2)}, u32[]{:S(2)}) collective-permute-start(bf16[512,768]{1,0:T(8,128)(2,1)} %dynamic-slice_bitcast_fusion), channel_id=1, source_target_pairs={{0,2},{1,3},{2,0},{3,1},{4,6},{5,7},{6,4},{7,5},{8,10},{9,11},{10,... | collective-permute-start | bytes 2359304 | tf_op jit(solution)/shard_map/ppermute | solution.py:25
  231.8 155.4 %collective-permute-start.4 = (bf16[512,768]{1,0:T(8,128)(2,1)}, bf16[512,768]{1,0:T(8,128)(2,1)}, u32[]{:S(2)}, u32[]{:S(2)}) collective-permute-start(bf16[512,768]{1,0:T(8,128)(2,1)} %dynamic-slice_bitcast_fusion.1), channel_id=1, source_target_pairs={{0,2},{1,3},{2,0},{3,1},{4,6},{5,7},{6,4},{7,5},{8,10},{9,11},{10,... | collective-permute-start | bytes 2359304 | tf_op jit(solution)/shard_map/ppermute | solution.py:25
  235.8 33.3 %collective-permute-start.8 = (bf16[1024,384]{1,0:T(8,128)(2,1)S(1)}, bf16[1024,384]{1,0:T(8,128)(2,1)S(1)}, u32[]{:S(2)}, u32[]{:S(2)}) collective-permute-start(bf16[1024,384]{1,0:T(8,128)(2,1)S(1)} %convolution_convert_fusion.3), channel_id=1, source_target_pairs={{0,1},{1,0},{2,3},{3,2},{4,5},{5,4},{6,7},{7,6},{8,9},{9,8},{10,11... | collective-permute-start | bytes 2359304 | tf_op jit(solution)/shard_map/ppermute | solution.py:25
  237.1 17.6 %collective-permute-start.33 = (bf16[384,768]{1,0:T(8,128)(2,1)S(1)}, bf16[384,768]{1,0:T(8,128)(2,1)S(1)}, u32[]{:S(2)}, u32[]{:S(2)}) collective-permute-start(bf16[384,768]{1,0:T(8,128)(2,1)S(1)} %convolution_convert_fusion.5), channel_id=1, source_target_pairs={{0,1},{1,0},{2,3},{3,2},{4,5},{5,4},{6,7},{7,6},{8,9},{9,8},{10,11... | collective-permute-start | bytes 1769480 | tf_op jit(solution)/shard_map/ppermute | solution.py:25
  238.7 290.7 %collective-permute-start.51 = (bf16[384,3072]{1,0:T(8,128)(2,1)}, bf16[384,3072]{1,0:T(8,128)(2,1)}, u32[]{:S(2)}, u32[]{:S(2)}) collective-permute-start(bf16[384,3072]{1,0:T(8,128)(2,1)} %constant_dynamic-slice_fusion.17), channel_id=1, source_target_pairs={{0,1},{1,0},{2,3},{3,2},{4,5},{5,4},{6,7},{7,6},{8,9},{9,8},{10,11... | collective-permute-start | bytes 7077896 | tf_op jit(solution)/shard_map/ppermute | solution.py:25
  239.3 15.4 %collective-permute-start.6 = (f32[15,768]{1,0:T(8,128)S(1)}, f32[15,768]{1,0:T(8,128)S(1)}, u32[]{:S(2)}, u32[]{:S(2)}) collective-permute-start(f32[15,768]{1,0:T(8,128)S(1)} %add_divide_fusion), channel_id=1, source_target_pairs={{0,2},{1,3},{2,0},{3,1},{4,6},{5,7},{6,4},{7,5},{8,10},{9,11},{10,... | collective-permute-start | bytes 138248 | tf_op jit(solution)/shard_map/ppermute | solution.py:25
  254.7 278.2 %collective-permute-start.69 = (bf16[1536,768]{1,0:T(8,128)(2,1)}, bf16[1536,768]{1,0:T(8,128)(2,1)}, u32[]{:S(2)}, u32[]{:S(2)}) collective-permute-start(bf16[1536,768]{1,0:T(8,128)(2,1)} %constant_dynamic-slice_fusion.8), channel_id=1, source_target_pairs={{0,1},{1,0},{2,3},{3,2},{4,5},{5,4},{6,7},{7,6},{8,9},{9,8},{10,11... | collective-permute-start | bytes 7077896 | tf_op jit(solution)/shard_map/ppermute | solution.py:25
  268.2 123.4 %collective-permute-start.43 = (bf16[96,384]{1,0:T(8,128)(2,1)}, bf16[96,384]{1,0:T(8,128)(2,1)}, u32[]{:S(2)}, u32[]{:S(2)}) collective-permute-start(bf16[96,384]{1,0:T(8,128)(2,1)} %constant_dynamic-slice_fusion.21), channel_id=1, source_target_pairs={{0,8},{4,12},{8,0},{12,4},{16,24},{20,28},{24,16},{28,20},{1,9},{5... | collective-permute-start | bytes 221192 | tf_op jit(solution)/shard_map/ppermute | solution.py:25
  269.1 123.9 %collective-permute-start.35 = (bf16[96,384]{1,0:T(8,128)(2,1)}, bf16[96,384]{1,0:T(8,128)(2,1)}, u32[]{:S(2)}, u32[]{:S(2)}) collective-permute-start(bf16[96,384]{1,0:T(8,128)(2,1)} %constant_dynamic-slice_fusion.26), channel_id=1, source_target_pairs={{0,4},{4,0},{8,12},{12,8},{16,20},{20,16},{24,28},{28,24},{1,5},{5... | collective-permute-start | bytes 221192 | tf_op jit(solution)/shard_map/ppermute | solution.py:25
  387.3 138.6 %collective-permute-start.9 = (bf16[2,512,768]{2,1,0:T(8,128)(2,1)}, bf16[2,512,768]{2,1,0:T(8,128)(2,1)}, u32[]{:S(2)}, u32[]{:S(2)}) collective-permute-start(bf16[2,512,768]{2,1,0:T(8,128)(2,1)} %fusion.13), channel_id=1, source_target_pairs={{0,1},{1,0},{2,3},{3,2},{4,5},{5,4},{6,7},{7,6},{8,9},{9,8},{10,11... | collective-permute-start | bytes 4718600 | tf_op jit(solution)/shard_map/ppermute | solution.py:25
  419.5 36.6 %collective-permute-start.19 = (bf16[384,576]{1,0:T(8,128)(2,1)}, bf16[384,576]{1,0:T(8,128)(2,1)}, u32[]{:S(2)}, u32[]{:S(2)}) collective-permute-start(bf16[384,576]{1,0:T(8,128)(2,1)} %constant_dynamic-slice_fusion.31), channel_id=1, source_target_pairs={{0,4},{4,0},{8,12},{12,8},{16,20},{20,16},{24,28},{28,24},{1,5},{5... | collective-permute-start | bytes 1327112 | tf_op jit(solution)/shard_map/ppermute | solution.py:25
  456.1 52.9 %collective-permute-start.50 = (bf16[384,768]{1,0:T(8,128)(2,1)S(1)}, bf16[384,768]{1,0:T(8,128)(2,1)S(1)}, u32[]{:S(2)}, u32[]{:S(2)}) collective-permute-start(bf16[384,768]{1,0:T(8,128)(2,1)S(1)} %maximum_maximum_fusion.3), channel_id=1, source_target_pairs={{0,1},{1,0},{2,3},{3,2},{4,5},{5,4},{6,7},{7,6},{8,9},{9,8},{10,11... | collective-permute-start | bytes 1769480 | tf_op jit(solution)/shard_map/ppermute | solution.py:25
  521.7 14.9 %collective-permute-start.26 = (bf16[384,576]{1,0:T(8,128)(2,1)S(1)}, bf16[384,576]{1,0:T(8,128)(2,1)S(1)}, u32[]{:S(2)}, u32[]{:S(2)}) collective-permute-start(bf16[384,576]{1,0:T(8,128)(2,1)S(1)} %pad_maximum_fusion.11), channel_id=1, source_target_pairs={{0,4},{4,0},{8,12},{12,8},{16,20},{20,16},{24,28},{28,24},{1,5},{5... | collective-permute-start | bytes 1327112 | tf_op jit(solution)/shard_map/ppermute | solution.py:25
  525.0 14.2 %collective-permute-start.18 = (bf16[384,576]{1,0:T(8,128)(2,1)S(1)}, bf16[384,576]{1,0:T(8,128)(2,1)S(1)}, u32[]{:S(2)}, u32[]{:S(2)}) collective-permute-start(bf16[384,576]{1,0:T(8,128)(2,1)S(1)} %pad_maximum_fusion.10), channel_id=1, source_target_pairs={{0,2},{1,3},{2,0},{3,1},{4,6},{5,7},{6,4},{7,5},{8,10},{9,11},{10,... | collective-permute-start | bytes 1327112 | tf_op jit(solution)/shard_map/ppermute | solution.py:25
  528.1 101.7 %collective-permute-start.10 = (bf16[512,768]{1,0:T(8,128)(2,1)S(1)}, bf16[512,768]{1,0:T(8,128)(2,1)S(1)}, u32[]{:S(2)}, u32[]{:S(2)}) collective-permute-start(bf16[512,768]{1,0:T(8,128)(2,1)S(1)} %fusion.19), channel_id=1, source_target_pairs={{0,2},{1,3},{2,0},{3,1},{4,6},{5,7},{6,4},{7,5},{8,10},{9,11},{10,... | collective-permute-start | bytes 2359304 | tf_op jit(solution)/shard_map/ppermute | solution.py:25
  532.9 22.1 %collective-permute-start.52 = (bf16[192,1536]{1,0:T(8,128)(2,1)S(1)}, bf16[192,1536]{1,0:T(8,128)(2,1)S(1)}, u32[]{:S(2)}, u32[]{:S(2)}) collective-permute-start(bf16[192,1536]{1,0:T(8,128)(2,1)S(1)} %constant_dynamic-slice_fusion.16), channel_id=1, source_target_pairs={{0,2},{1,3},{2,0},{3,1},{4,6},{5,7},{6,4},{7,5},{8,10},{9,11},{10,... | collective-permute-start | bytes 1769480 | tf_op jit(solution)/shard_map/ppermute | solution.py:25
  536.7 19.9 %collective-permute-start.78 = (bf16[768,384]{1,0:T(8,128)(2,1)S(1)}, bf16[768,384]{1,0:T(8,128)(2,1)S(1)}, u32[]{:S(2)}, u32[]{:S(2)}) collective-permute-start(bf16[768,384]{1,0:T(8,128)(2,1)S(1)} %constant_dynamic-slice_fusion.3), channel_id=1, source_target_pairs={{0,4},{4,0},{8,12},{12,8},{16,20},{20,16},{24,28},{28,24},{1,5},{5... | collective-permute-start | bytes 1769480 | tf_op jit(solution)/shard_map/ppermute | solution.py:25
  539.3 22.3 %collective-permute-start.70 = (bf16[768,384]{1,0:T(8,128)(2,1)S(1)}, bf16[768,384]{1,0:T(8,128)(2,1)S(1)}, u32[]{:S(2)}, u32[]{:S(2)}) collective-permute-start(bf16[768,384]{1,0:T(8,128)(2,1)S(1)} %constant_dynamic-slice_fusion.7), channel_id=1, source_target_pairs={{0,2},{1,3},{2,0},{3,1},{4,6},{5,7},{6,4},{7,5},{8,10},{9,11},{10,... | collective-permute-start | bytes 1769480 | tf_op jit(solution)/shard_map/ppermute | solution.py:25
  542.3 104.7 %collective-permute-start.27 = (bf16[768,1152]{1,0:T(8,128)(2,1)S(1)}, bf16[768,1152]{1,0:T(8,128)(2,1)S(1)}, u32[]{:S(2)}, u32[]{:S(2)}) collective-permute-start(bf16[768,1152]{1,0:T(8,128)(2,1)S(1)} %maximum_maximum_fusion.2), channel_id=1, source_target_pairs={{0,1},{1,0},{2,3},{3,2},{4,5},{5,4},{6,7},{7,6},{8,9},{9,8},{10,11... | collective-permute-start | bytes 5308424 | tf_op jit(solution)/shard_map/ppermute | solution.py:25
  613.4 15.2 %collective-permute-start.76 = (bf16[384,384]{1,0:T(8,128)(2,1)S(1)}, bf16[384,384]{1,0:T(8,128)(2,1)S(1)}, u32[]{:S(2)}, u32[]{:S(2)}) collective-permute-start(bf16[384,384]{1,0:T(8,128)(2,1)S(1)} %pad_maximum_fusion.14), channel_id=1, source_target_pairs={{0,4},{4,0},{8,12},{12,8},{16,20},{20,16},{24,28},{28,24},{1,5},{5... | collective-permute-start | bytes 884744 | tf_op jit(solution)/shard_map/ppermute | solution.py:25
  628.5 24.1 %collective-permute-start.68 = (bf16[384,3072]{1,0:T(8,128)(2,1)S(1)}, bf16[384,3072]{1,0:T(8,128)(2,1)S(1)}, u32[]{:S(2)}, u32[]{:S(2)}) collective-permute-start(bf16[384,3072]{1,0:T(8,128)(2,1)S(1)} %maximum_maximum_fusion), channel_id=1, source_target_pairs={{0,1},{1,0},{2,3},{3,2},{4,5},{5,4},{6,7},{7,6},{8,9},{9,8},{10,11... | collective-permute-start | bytes 7077896 | tf_op jit(solution)/shard_map/ppermute | solution.py:25
  628.8 15.8 %collective-permute-start.77 = (bf16[768,384]{1,0:T(8,128)(2,1)S(1)}, bf16[768,384]{1,0:T(8,128)(2,1)S(1)}, u32[]{:S(2)}, u32[]{:S(2)}) collective-permute-start(bf16[768,384]{1,0:T(8,128)(2,1)S(1)} %pad_maximum_fusion.8), channel_id=1, source_target_pairs={{0,2},{1,3},{2,0},{3,1},{4,6},{5,7},{6,4},{7,5},{8,10},{9,11},{10,... | collective-permute-start | bytes 1769480 | tf_op jit(solution)/shard_map/ppermute | solution.py:25
  645.0 22.9 %collective-permute-start.86 = (bf16[1536,768]{1,0:T(8,128)(2,1)S(1)}, bf16[1536,768]{1,0:T(8,128)(2,1)S(1)}, u32[]{:S(2)}, u32[]{:S(2)}) collective-permute-start(bf16[1536,768]{1,0:T(8,128)(2,1)S(1)} %maximum_maximum_fusion.1), channel_id=1, source_target_pairs={{0,1},{1,0},{2,3},{3,2},{4,5},{5,4},{6,7},{7,6},{8,9},{9,8},{10,11... | collective-permute-start | bytes 7077896 | tf_op jit(solution)/shard_map/ppermute | solution.py:25
  (116 other events, 1050.4 us)

commit v2 on v1

v2 whole, which is shorter than its diff:
```python
import jax
import jax.numpy as jnp
from jax import lax
from jax.experimental import pallas as pl
from jax.experimental.pallas import tpu as pltpu
from jax.sharding import PartitionSpec as P

HD = 64
NSENT = 15
SLOTS = 16
LONGEST = 1024
EPS = 1e-06
PAIR = 2 * HD
GRAIN = 128
QB = 256
KB = 256
TB = 256
MASKED = -1e30
BF16 = jnp.bfloat16
F32 = jnp.float32
NN = ((1,), (0,))
NT = ((1,), (1,))
TN = ((0,), (0,))


def swap(value, axis, bit):
    size = lax.axis_size(axis)
    return lax.ppermute(value, axis, [(i, i ^ bit) for i in range(size)])


def bit_of(axis, bit):
    return (lax.axis_index(axis) // bit) % 2


def dot(left, right, contract):
    return lax.dot_general(left, right, (contract, ((), ())), preferred_element_type=F32)


def whole(shape):
    return pl.BlockSpec(shape, lambda *_: (0,) * len(shape), pipeline_mode=pl.Buffered(1))


def params(mib):
    return pltpu.CompilerParams(vmem_limit_bytes=mib << 20)


def cost(flops, moved, exps=0):
    return pl.CostEstimate(flops=flops, bytes_accessed=moved, transcendentals=exps)


def shifted(source_ref, start, count):
    base = pl.multiple_of((start // 16) * 16, 16)
    row = lax.broadcasted_iota(jnp.int32, (count, count + GRAIN), 0)
    column = lax.broadcasted_iota(jnp.int32, (count, count + GRAIN), 1)
    select = (column == row + (start - base)).astype(BF16)
    return dot(select, source_ref[pl.ds(base, count + GRAIN), :], NN).astype(BF16)


def wrap(ref, length):
    ref[length : length + QB + GRAIN, :] = ref[: QB + GRAIN, :]


def project_kernel(info_ref, a_ref, b_ref, c_ref, d_ref, weight_ref, bias_ref, scale_ref, x_ref, out_ref, row_ref):
    step = pl.program_id(0)
    chunk = a_ref.shape[0]
    length = 4 * chunk

    @pl.when(step == 0)
    def _():
        for slot, source in enumerate((a_ref, b_ref, c_ref, d_ref)):
            row_ref[pl.ds(pl.multiple_of(info_ref[1 + slot] * chunk, chunk), chunk), :] = source[...]
        wrap(row_ref, length)

    part = shifted(row_ref, (info_ref[0] + step * QB) % length, QB)
    x_ref[...] = part
    out_ref[...] = ((dot(part, weight_ref[...], NN) + bias_ref[...]) * scale_ref[...]).astype(BF16)


def project(info, chunks, weight, bias, scale):
    chunk, width = chunks[0].shape
    columns = weight.shape[1]
    length = 4 * chunk
    return pl.pallas_call(
        project_kernel,
        grid_spec=pltpu.PrefetchScalarGridSpec(
            num_scalar_prefetch=1,
            grid=(length // QB,),
            in_specs=[whole((chunk, width))] * 4 + [whole((width, columns)), whole((1, columns)), whole((1, columns))],
            out_specs=[
                pl.BlockSpec((QB, width), lambda i, _: (i, 0)),
                pl.BlockSpec((QB, columns), lambda i, _: (i, 0)),
            ],
            scratch_shapes=[pltpu.VMEM((length + QB + GRAIN, width), BF16)],
        ),
        out_shape=[jax.ShapeDtypeStruct((length, width), BF16), jax.ShapeDtypeStruct((length, columns), BF16)],
        compiler_params=params(40),
        cost_estimate=cost(2 * length * width * (columns + QB), 14 * length * width),
        name="project",
    )(info, *chunks, weight, bias, scale)


def stack_heads(block, feature=None):
    lane = lax.broadcasted_iota(jnp.int32, block.shape, 1)
    zero = jnp.zeros_like(block)
    first, second = jnp.where(lane < HD, block, zero), jnp.where(lane < HD, zero, block)
    if feature is not None:
        first = jnp.concatenate([first, feature], axis=1)
        second = jnp.concatenate([second, feature], axis=1)
    return jnp.concatenate([first, second], axis=0)


def merge_heads(stacked):
    first, second = stacked[:QB], stacked[QB:]
    lane = lax.broadcasted_iota(jnp.int32, first.shape, 1)
    return jnp.where(lane < HD, first, second)


def fold(block, how):
    return how(block.reshape(block.shape[0] // 8, 8, block.shape[1]), axis=0)


def attend_kernel(info_ref, packed_ref, qf_ref, kf_ref, rolled_ref, keep_ref, send_ref, lse_ref, score_ref, acc_ref, row_ref):
    length = packed_ref.shape[0]
    pairs = packed_ref.shape[1] // (3 * PAIR)
    column = lambda pair, part: slice((3 * pair + part) * PAIR, (3 * pair + part + 1) * PAIR)
    lanes = lambda pair: slice(pair * PAIR, (pair + 1) * PAIR)
    stats = lambda pair: slice(pair * 2 * QB, (pair + 1) * 2 * QB)

    def weigh(pair, keys, scores, top):
        soft = jnp.exp(scores - top)
        value = packed_ref[keys, column(pair, 2)]
        side = jnp.concatenate([value, jnp.ones_like(value)], axis=1)
        return dot(soft.astype(BF16), side, TN), fold(soft, jnp.sum)

    def finish(block, rows, pair, top, total, acc):
        total = jnp.sum(total, axis=0, keepdims=True)
        lse_ref[pl.ds(block, 1), stats(pair)] = top + jnp.log(total)
        row_ref[rows, lanes(pair)] = merge_heads(acc[:, :PAIR] / acc[:, PAIR:]).astype(BF16)

    @pl.loop(0, LONGEST // QB)
    def _(block):
        rows = pl.ds(pl.multiple_of(block * QB, QB), QB)
        size = LONGEST // 2
        tops = {}

        def look(pair, k):
            stacked = stack_heads(packed_ref[rows, column(pair, 0)])
            score = dot(packed_ref[k : k + size, column(pair, 1)], stacked, NT)
            score_ref[pair, k : k + size, :] = score
            top = fold(score, jnp.max)
            tops[pair] = top if k == 0 else jnp.maximum(tops[pair], top)

        for k in (0, size):
            look(0, k)
        for pair in range(pairs):
            top = jnp.max(tops[pair], axis=0, keepdims=True)
            acc = total = None
            for k in (0, size):
                if pair + 1 < pairs:
                    look(pair + 1, k)
                more, add = weigh(pair, slice(k, k + size), score_ref[pair, k : k + size, :], top)
                acc = more if acc is None else acc + more
                total = add if total is None else total + add
            finish(block, rows, pair, top, total, acc)

    @pl.loop(LONGEST // QB, length // QB)
    def _(block):
        rows = pl.ds(pl.multiple_of(block * QB, QB), QB)
        start = info_ref[1 + block] * GRAIN
        count = info_ref[1 + length // QB + block]
        stacked = [stack_heads(packed_ref[rows, column(pair, 0)], qf_ref[rows, :]) for pair in range(pairs)]

        def look(j, tops):
            keys = pl.ds(pl.multiple_of(start + j * KB, GRAIN), KB)
            found = []
            for pair in range(pairs):
                side = jnp.concatenate([packed_ref[keys, column(pair, 1)], kf_ref[keys, :]], axis=1)
                score = dot(side, stacked[pair], NT)
                score_ref[pair, pl.ds(pl.multiple_of(j * KB, KB), KB), :] = score
                found.append(jnp.maximum(tops[pair], fold(score, jnp.max)))
            return tuple(found)

        tops = lax.fori_loop(0, count, look, (jnp.full((8, 2 * QB), -jnp.inf, F32),) * pairs)
        tops = [jnp.max(top, axis=0, keepdims=True) for top in tops]
        acc_ref[...] = jnp.zeros_like(acc_ref)

        def take(j, totals):
            keys = pl.ds(pl.multiple_of(start + j * KB, GRAIN), KB)
            found = []
            for pair in range(pairs):
                scores = score_ref[pair, pl.ds(pl.multiple_of(j * KB, KB), KB), :]
                more, add = weigh(pair, keys, scores, tops[pair])
                acc_ref[pair] += more
                found.append(totals[pair] + add)
            return tuple(found)

        totals = lax.fori_loop(0, count, take, (jnp.zeros((8, 2 * QB), F32),) * pairs)
        for pair in range(pairs):
            finish(block, rows, pair, tops[pair], totals[pair], acc_ref[pair])

    rolled_ref[...] = row_ref[:length, :]
    wrap(row_ref, length)
    chunk = length // 4
    for block in range(length // QB):
        part = shifted(row_ref, (block * QB - info_ref[0] + length) % length, QB)
        place, inside = divmod(block * QB, chunk)
        rows = slice(place // 2 * chunk + inside, place // 2 * chunk + inside + QB)
        own = info_ref[1 + 2 * (length // QB)] == place % 2

        @pl.when(own)
        def _(part=part, rows=rows):
            keep_ref[rows, :] = part

        @pl.when(jnp.logical_not(own))
        def _(part=part, rows=rows):
            send_ref[rows, :] = part


def attend(info, packed, query_feature, key_feature):
    length, columns = packed.shape
    width = columns // 3
    pairs = width // PAIR
    tokens = jax.ShapeDtypeStruct((length // 2, width), BF16)
    shapes = [
        jax.ShapeDtypeStruct((length, width), BF16),
        tokens,
        tokens,
        jax.ShapeDtypeStruct((length // QB, 2 * pairs * QB), F32),
    ]
    return pl.pallas_call(
        attend_kernel,
        grid_spec=pltpu.PrefetchScalarGridSpec(
            num_scalar_prefetch=1,
            grid=(1,),
            in_specs=[whole((length, columns)), whole((length, PAIR)), whole((length, PAIR))],
            out_specs=[whole(s.shape) for s in shapes],
            scratch_shapes=[
                pltpu.VMEM((pairs, length // 2, 2 * QB), F32),
                pltpu.VMEM((pairs, 2 * QB, 2 * PAIR), F32),
                pltpu.VMEM((length + QB + GRAIN, width), BF16),
            ],
        ),
        out_shape=shapes,
        compiler_params=params(48),
        cost_estimate=cost(6 * length * length * width, 12 * length * width, length * length),
        name="attend",
    )(info, packed, query_feature, key_feature)


def roll_back_kernel(info_ref, mine_ref, came_ref, rolled_ref, out_ref, delta_ref, row_ref):
    length, width = out_ref.shape
    chunk = length // 4
    for half in range(2):
        own = pl.multiple_of((2 * half + info_ref[1]) * chunk, chunk)
        other = pl.multiple_of((2 * half + 1 - info_ref[1]) * chunk, chunk)
        row_ref[pl.ds(own, chunk), :] = mine_ref[half * chunk : (half + 1) * chunk, :]
        row_ref[pl.ds(other, chunk), :] = came_ref[half * chunk : (half + 1) * chunk, :]
    wrap(row_ref, length)
    for block in range(length // QB):
        rows = slice(block * QB, (block + 1) * QB)
        part = shifted(row_ref, (block * QB + info_ref[0]) % length, QB)
        out_ref[rows, :] = part
        product = part.astype(F32) * rolled_ref[rows, :].astype(F32)
        for head in range(width // HD):
            if head % 2 == 0:
                turned = product[:, head * HD : head * HD + PAIR].T
            line = jnp.sum(turned[head % 2 * HD : (head % 2 + 1) * HD], axis=0, keepdims=True)
            delta_ref[block : block + 1, head * QB : (head + 1) * QB] = line


def roll_back(info, mine, came, rolled):
    length, width = rolled.shape
    shapes = [
        jax.ShapeDtypeStruct((length, width), BF16),
        jax.ShapeDtypeStruct((length // QB, width // HD * QB), F32),
    ]
    return pl.pallas_call(
        roll_back_kernel,
        grid_spec=pltpu.PrefetchScalarGridSpec(
            num_scalar_prefetch=1,
            grid=(1,),
            in_specs=[whole(mine.shape), whole(came.shape), whole(rolled.shape)],
            out_specs=[whole(s.shape) for s in shapes],
            scratch_shapes=[pltpu.VMEM((length + QB + GRAIN, width), BF16)],
        ),
        out_shape=shapes,
        compiler_params=params(32),
        cost_estimate=cost(2 * length * width * QB, 8 * length * width),
        name="roll_back",
    )(info, mine, came, rolled)


def back_step(key, side, stacked, queries, ups, value, lse, delta):
    soft = jnp.exp(dot(side, stacked, NT) - lse)
    d_soft = dot(value, ups, NT)
    d_score = (soft * (d_soft - delta)).astype(BF16)
    return dot(d_score, queries, NN), dot(soft.astype(BF16), ups, NN), dot(d_score, key, TN)


def long_back_kernel(packed_ref, up_ref, lse_ref, delta_ref, out_ref, dk_acc, dv_acc):
    dk_acc[...] = jnp.zeros_like(dk_acc)
    dv_acc[...] = jnp.zeros_like(dv_acc)
    size = LONGEST // 2

    @pl.loop(0, LONGEST // QB)
    def _(block):
        rows = pl.ds(pl.multiple_of(block * QB, QB), QB)
        queries = stack_heads(packed_ref[rows, :PAIR])
        ups = stack_heads(up_ref[rows, :])
        lse, delta = lse_ref[pl.ds(block, 1), :], delta_ref[pl.ds(block, 1), :]
        dq = None
        for k in (0, size):
            keys = slice(k, k + size)
            key = packed_ref[keys, PAIR : 2 * PAIR]
            dk, dv, more = back_step(key, key, queries, queries, ups, packed_ref[keys, 2 * PAIR :], lse, delta)
            dk_acc[keys, :] += dk
            dv_acc[keys, :] += dv
            dq = more if dq is None else dq + more
        out_ref[rows, :PAIR] = (merge_heads(dq) * 0.125).astype(BF16)

    out_ref[:, PAIR : 2 * PAIR] = dk_acc[...].astype(BF16)
    out_ref[:, 2 * PAIR :] = dv_acc[...].astype(BF16)


def long_back(pair, packed, upstream, lse, delta):
    at = lambda *shape: pl.BlockSpec(shape, lambda i: (0, pair), pipeline_mode=pl.Buffered(1))
    blocks = packed.shape[0] // QB
    return pl.pallas_call(
        long_back_kernel,
        grid=(1,),
        in_specs=[at(LONGEST, 3 * PAIR), at(LONGEST, PAIR), at(blocks, 2 * QB), at(blocks, 2 * QB)],
        out_specs=whole((LONGEST, 3 * PAIR)),
        scratch_shapes=[pltpu.VMEM((LONGEST, PAIR), F32)] * 2,
        out_shape=jax.ShapeDtypeStruct((LONGEST, 3 * PAIR), BF16),
        compiler_params=params(40),
        cost_estimate=cost(40 * LONGEST * LONGEST * PAIR, 16 * LONGEST * PAIR, LONGEST * LONGEST),
        name="long_back",
    )(packed, upstream, lse, delta)


def rest_back_kernel(info_ref, packed_ref, up_ref, lse_ref, delta_ref, qf_ref, kf_ref, out_ref, dk_acc, dv_acc, dq_acc):
    length, pairs = packed_ref.shape[0], packed_ref.shape[1] // (3 * PAIR)
    first, blocks = LONGEST // QB, (length + LONGEST) // QB
    column = lambda pair, part: slice((3 * pair + part) * PAIR, (3 * pair + part + 1) * PAIR)
    lanes = lambda pair: slice(pair * PAIR, (pair + 1) * PAIR)
    stats = lambda pair: slice(pair * 2 * QB, (pair + 1) * 2 * QB)
    dk_acc[...] = jnp.zeros_like(dk_acc)
    dv_acc[...] = jnp.zeros_like(dv_acc)

    @pl.loop(0, length // QB)
    def _(block):
        rows = pl.ds(pl.multiple_of(block * QB, QB), QB)
        start = info_ref[1 + first + block] * GRAIN - LONGEST
        count = info_ref[1 + blocks + first + block]
        feature = qf_ref[rows, :]
        ready = []
        for pair in range(pairs):
            query = packed_ref[rows, column(pair, 0)]
            line = pl.ds(first + block, 1)
            ready.append(
                (
                    stack_heads(query, feature),
                    stack_heads(query),
                    stack_heads(up_ref[rows, lanes(pair)]),
                    lse_ref[line, stats(pair)],
                    delta_ref[line, stats(pair)],
                )
            )
        dq_acc[...] = jnp.zeros_like(dq_acc)

        @pl.loop(0, count)
        def _(j):
            keys = pl.ds(pl.multiple_of(start + j * KB, GRAIN), KB)
            for pair in range(pairs):
                stacked, queries, ups, lse, delta = ready[pair]
                key = packed_ref[keys, column(pair, 1)]
                side = jnp.concatenate([key, kf_ref[keys, :]], axis=1)
                dk, dv, dq = back_step(key, side, stacked, queries, ups, packed_ref[keys, column(pair, 2)], lse, delta)
                dk_acc[keys, lanes(pair)] += dk
                dv_acc[keys, lanes(pair)] += dv
                dq_acc[pair] += dq

        for pair in range(pairs):
            out_ref[rows, column(pair, 0)] = (merge_heads(dq_acc[pair]) * 0.125).astype(BF16)

    for pair in range(pairs):
        out_ref[:, column(pair, 1)] = dk_acc[:, lanes(pair)].astype(BF16)
        out_ref[:, column(pair, 2)] = dv_acc[:, lanes(pair)].astype(BF16)


def rest_back(info, packed, upstream, lse, delta, query_feature, key_feature):
    length, columns = packed.shape
    rest, width = length - LONGEST, columns // 3
    pairs = width // PAIR
    later = lambda w: pl.BlockSpec((rest, w), lambda i, _: (1, 0), pipeline_mode=pl.Buffered(1))
    return pl.pallas_call(
        rest_back_kernel,
        grid_spec=pltpu.PrefetchScalarGridSpec(
            num_scalar_prefetch=1,
            grid=(1,),
            in_specs=[later(columns), later(width), whole(lse.shape), whole(delta.shape), later(PAIR), later(PAIR)],
            out_specs=whole((rest, columns)),
            scratch_shapes=[
                pltpu.VMEM((rest, width), F32),
                pltpu.VMEM((rest, width), F32),
                pltpu.VMEM((pairs, 2 * QB, PAIR), F32),
            ],
        ),
        out_shape=jax.ShapeDtypeStruct((rest, columns), BF16),
        compiler_params=params(40),
        cost_estimate=cost(24 * rest * rest * width, 16 * rest * width, rest * rest),
        name="rest_back",
    )(info, packed, upstream, lse, delta, query_feature, key_feature)


def input_grad_kernel(info_ref, *refs):
    pieces, rest_ref, weight_ref, keep_ref, send_ref, row_ref = refs[:-5], *refs[-5:]
    length = row_ref.shape[0] - QB - GRAIN
    width = 3 * PAIR
    for block in range(LONGEST // QB):
        rows = slice(block * QB, (block + 1) * QB)
        total = None
        for pair, piece in enumerate(pieces):
            more = dot(piece[rows, :], weight_ref[:, pair * width : (pair + 1) * width], NT)
            total = more if total is None else total + more
        row_ref[rows, :] = total.astype(BF16)
    for block in range(rest_ref.shape[0] // QB):
        rows = slice(block * QB, (block + 1) * QB)
        row_ref[LONGEST + block * QB : LONGEST + (block + 1) * QB, :] = dot(rest_ref[rows, :], weight_ref[...], NT).astype(BF16)
    wrap(row_ref, length)
    chunk = length // 4
    for block in range(length // QB):
        part = shifted(row_ref, (block * QB - info_ref[0] + length) % length, QB)
        place, inside = divmod(block * QB, chunk)
        rows = slice(place // 2 * chunk + inside, place // 2 * chunk + inside + QB)
        own = info_ref[1] == place % 2

        @pl.when(own)
        def _(part=part, rows=rows):
            keep_ref[rows, :] = part

        @pl.when(jnp.logical_not(own))
        def _(part=part, rows=rows):
            send_ref[rows, :] = part


def input_grad(info, pieces, rest, weight):
    width, columns = weight.shape
    length = LONGEST + rest.shape[0]
    tokens = jax.ShapeDtypeStruct((length // 2, width), BF16)
    return pl.pallas_call(
        input_grad_kernel,
        grid_spec=pltpu.PrefetchScalarGridSpec(
            num_scalar_prefetch=1,
            grid=(1,),
            in_specs=[whole(p.shape) for p in pieces] + [whole(rest.shape), whole(weight.shape)],
            out_specs=[whole(tokens.shape)] * 2,
            scratch_shapes=[pltpu.VMEM((length + QB + GRAIN, width), BF16)],
        ),
        out_shape=[tokens, tokens],
        compiler_params=params(40),
        cost_estimate=cost(2 * length * width * (columns + QB), 8 * length * width),
        name="input_grad",
    )(info, *pieces, rest, weight)


def gelu_both(value):
    cdf = 0.5 * lax.erf(value * 0.7071067811865476) + 0.5
    return value * cdf, cdf + value * (jnp.exp(value * value * -0.5) * 0.3989422804014327)


def normalise(value):
    centred = value - jnp.mean(value, axis=-1, keepdims=True)
    rate = lax.rsqrt(jnp.mean(centred * centred, axis=-1, keepdims=True) + EPS)
    return centred * rate, rate


def normalise_back(upstream, normal, rate, gain):
    scaled = upstream * gain
    first = jnp.mean(scaled, axis=-1, keepdims=True)
    second = jnp.mean(scaled * normal, axis=-1, keepdims=True)
    return rate * (scaled - first - normal * second)


def rows_sum(value):
    return jnp.sum(value, axis=0, keepdims=True)


def tokens_kernel(
    info_ref, mine_ref, other_ref, xa_ref, xb_ref, ca_ref, cb_ref, member_ref, pool_weight_ref,
    out_mine_ref, out_other_ref, up_ref, down_ref, vector_ref, up_bias_ref,
    out_ref, act_ref, branch_ref, normed_ref, pre_ref, attn_ref, first_ref, d_mine_ref, d_other_ref,
    pool_ref, small_ref, up_small_ref, slope_ref,
):
    step = pl.program_id(0)
    half = pl.num_programs(0) // 2

    @pl.when(step == 0)
    def _():
        pool_ref[...] = jnp.zeros_like(pool_ref)
        small_ref[...] = jnp.zeros_like(small_ref)
        up_small_ref[...] = jnp.zeros_like(up_small_ref)

    out_bias, gain_one, shift_one, down_bias, gain_two, shift_two = [vector_ref[k : k + 1, :] for k in range(6)]
    hidden = up_ref.shape[1]
    width = vector_ref.shape[1]
    own = info_ref[0] == step // half
    inputs = jnp.where(own, xa_ref[...], xb_ref[...]).astype(F32)
    first_sum = inputs + dot(mine_ref[...], out_mine_ref[...], NN) + dot(other_ref[...], out_other_ref[...], NN) + out_bias
    normal_one, rate_one = normalise(first_sum)
    normed = normal_one * gain_one + shift_one
    normed_low = normed.astype(BF16)
    normed_ref[...] = normed_low
    second_sum = normed + down_bias
    for c in range(0, hidden, width):
        cols = slice(c, c + width)
        act, slope = gelu_both(dot(normed_low, up_ref[:, cols], NN) + up_bias_ref[:, cols])
        act = act.astype(BF16)
        act_ref[:, cols] = act
        slope_ref[:, cols] = slope
        second_sum = second_sum + dot(act, down_ref[cols, :], NN)
    normal_two, rate_two = normalise(second_sum)
    final = (normal_two * gain_two + shift_two).astype(BF16)
    out_ref[...] = final
    member = member_ref[...]
    pool_ref[...] += dot(member, final, TN)[:SLOTS]
    upstream = jnp.where(own, ca_ref[...], cb_ref[...]).astype(F32)
    upstream = upstream + dot(jnp.concatenate([member, member], axis=1), pool_weight_ref[...], NN)
    d_second = normalise_back(upstream, normal_two, rate_two, gain_two)
    branch = d_second.astype(BF16)
    branch_ref[...] = branch
    d_normed = d_second
    for c in range(0, hidden, width):
        cols = slice(c, c + width)
        pre = (dot(branch, down_ref[cols, :], NT) * slope_ref[:, cols]).astype(BF16)
        pre_ref[:, cols] = pre
        up_small_ref[:, cols] += rows_sum(pre.astype(F32))
        d_normed = d_normed + dot(pre, up_ref[:, cols], NT)
    first = normalise_back(d_normed, normal_one, rate_one, gain_one)
    first_ref[...] = first
    attn = first.astype(BF16)
    attn_ref[...] = attn
    d_mine_ref[...] = dot(attn, out_mine_ref[...], NT).astype(BF16)
    d_other_ref[...] = dot(attn, out_other_ref[...], NT).astype(BF16)
    small_ref[...] += jnp.concatenate(
        [
            rows_sum(attn.astype(F32)),
            rows_sum(d_normed * normal_one),
            rows_sum(d_normed),
            rows_sum(branch.astype(F32)),
            rows_sum(upstream * normal_two),
            rows_sum(upstream),
            jnp.zeros((2, width), F32),
        ],
        axis=0,
    )


def token_layers(info, mine, other, own, came, cot_own, cot_came, member, pool_weight, out_mine, out_other, up, down, vectors, up_bias):
    count, head_width = mine.shape
    width, hidden = up.shape
    chunk = own.shape[0]
    per = chunk // TB
    token = lambda w: pl.BlockSpec((TB, w), lambda i, _: (i, 0))
    piece = pl.BlockSpec((TB, width), lambda i, _: (i % per, 0))
    placed = pl.BlockSpec((TB, PAIR), lambda i, info: (info[1 + i // per] * per + i % per, 0))
    tokens = [
        (width, BF16), (hidden, BF16), (width, BF16), (width, BF16), (hidden, BF16), (width, BF16), (width, F32),
        (head_width, BF16), (head_width, BF16),
    ]
    sums = [(SLOTS, width), (8, width), (1, hidden)]
    held = lambda shape: pl.BlockSpec(shape, lambda i, _: (0, 0))
    return pl.pallas_call(
        tokens_kernel,
        grid_spec=pltpu.PrefetchScalarGridSpec(
            num_scalar_prefetch=1,
            grid=(count // TB,),
            in_specs=[token(head_width), token(head_width), piece, piece, piece, piece, placed]
            + [whole(a.shape) for a in (pool_weight, out_mine, out_other, up, down, vectors, up_bias)],
            out_specs=[token(w) for w, _ in tokens] + [held(s) for s in sums],
            scratch_shapes=[pltpu.VMEM((TB, hidden), F32)],
        ),
        out_shape=[jax.ShapeDtypeStruct((count, w), d) for w, d in tokens] + [jax.ShapeDtypeStruct(s, F32) for s in sums],
        compiler_params=params(58),
        cost_estimate=cost(4 * count * width * (2 * hidden + width), 8 * width * hidden + 40 * count * width, 2 * count * hidden),
        name="token_layers",
    )(info, mine, other, own, came, cot_own, cot_came, member, pool_weight, out_mine, out_other, up, down, vectors, up_bias)


def product_kernel(add, info_ref, left_ref, right_ref, *refs):
    total = dot(left_ref[...], right_ref[...], TN)
    if add:
        total = total + refs[0][...].astype(F32)
    refs[-1][...] = total.astype(BF16)


def product(side, left, right, there=None):
    count, rows = left.shape
    columns = right.shape[1]
    wide = min(rows, columns)
    panels = max(rows, columns) // wide // 2
    moved = pl.BlockSpec((count, wide), lambda i, info: (0, info[0] * panels + i))
    out = pl.BlockSpec((wide, wide), lambda i, _: (i, 0))
    extra = [] if there is None else [there]
    return pl.pallas_call(
        lambda *refs: product_kernel(bool(extra), *refs),
        grid_spec=pltpu.PrefetchScalarGridSpec(
            num_scalar_prefetch=1,
            grid=(panels,),
            in_specs=[
                moved if rows > columns else whole(left.shape),
                moved if columns > rows else whole(right.shape),
            ]
            + [out] * len(extra),
            out_specs=out,
        ),
        out_shape=jax.ShapeDtypeStruct((panels * wide, wide), BF16),
        compiler_params=params(40),
        cost_estimate=cost(2 * count * panels * wide * wide, 2 * count * (panels + 1) * wide),
        name="product",
    )(side, left, right, *extra)


def head_product_kernel(add, left_ref, right_ref, *refs):
    total = dot(left_ref[...], right_ref[...], TN)
    if add:
        total = total + refs[0][...].astype(F32)
    refs[-1][...] = total.astype(BF16)


def head_product(left, right, there=None):
    extra = [] if there is None else [there]
    shape = (left.shape[1], right.shape[1])
    return pl.pallas_call(
        lambda *refs: head_product_kernel(bool(extra), *refs),
        out_shape=jax.ShapeDtypeStruct(shape, BF16),
        compiler_params=params(32),
        cost_estimate=cost(2 * left.size * right.shape[1], 4 * left.size),
        name="head_product",
    )(left, right, *extra)


def packed_product_kernel(bit_ref, x_ref, *refs):
    pairs = (len(refs) - 2) // 3
    pieces, rest_ref, outs, bias_ref = refs[:pairs], refs[pairs], refs[pairs + 1 : -1], refs[-1]
    width = 3 * PAIR
    for pair, piece in enumerate(pieces):
        columns = slice(pair * width, (pair + 1) * width)
        later = rest_ref[:, columns]
        total = dot(x_ref[:LONGEST, :], piece[...], TN) + dot(x_ref[LONGEST:, :], later, TN)
        half = total.shape[0] // 2
        upper = bit_ref[pair] == 1
        outs[2 * pair][...] = jnp.where(upper, total[half:], total[:half]).astype(BF16)
        outs[2 * pair + 1][...] = jnp.where(upper, total[:half], total[half:]).astype(BF16)
        bias_ref[:, columns] = rows_sum(piece[...].astype(F32)) + rows_sum(later.astype(F32))


def packed_product(bits, rolled, pieces, rest):
    length, width = rolled.shape
    part = jax.ShapeDtypeStruct((width // 2, 3 * PAIR), BF16)
    shapes = [part] * (2 * len(pieces)) + [jax.ShapeDtypeStruct((1, rest.shape[1]), F32)]
    return pl.pallas_call(
        packed_product_kernel,
        grid_spec=pltpu.PrefetchScalarGridSpec(
            num_scalar_prefetch=1,
            grid=(1,),
            in_specs=[whole(rolled.shape)] + [whole(p.shape) for p in pieces] + [whole(rest.shape)],
            out_specs=[whole(s.shape) for s in shapes],
        ),
        out_shape=shapes,
        compiler_params=params(40),
        cost_estimate=cost(2 * length * width * rest.shape[1], 8 * length * width),
        name="packed_product",
    )(bits, rolled, *pieces, rest)


def split_kernel(bit_ref, down_ref, up_ref, out_ref, *refs):
    cut = refs[0].shape[0] * 2
    tail = down_ref.shape[0] - cut
    head = out_ref.shape[0]
    for part, source in enumerate((down_ref, up_ref)):
        upper = bit_ref[part] == 1
        lower_half, upper_half = source[: cut // 2, :], source[cut // 2 : cut, :]
        refs[2 * part][...] = jnp.where(upper, upper_half, lower_half)
        refs[2 * part + 1][...] = jnp.where(upper, lower_half, upper_half)
    upper = bit_ref[2] == 1
    last = jnp.concatenate([down_ref[cut:, :], up_ref[cut:, :], out_ref[...]], axis=0)
    half = (2 * tail + head) // 2
    refs[4][...] = jnp.where(upper, last[half:], last[:half])
    refs[5][...] = jnp.where(upper, last[:half], last[half:])


def split(bits, down, up, out):
    third = (down.shape[0] + up.shape[0] + out.shape[0]) // 3
    shape = jax.ShapeDtypeStruct((third // 2, down.shape[1]), BF16)
    return pl.pallas_call(
        split_kernel,
        grid_spec=pltpu.PrefetchScalarGridSpec(
            num_scalar_prefetch=1,
            grid=(1,),
            in_specs=[whole(down.shape), whole(up.shape), whole(out.shape)],
            out_specs=[whole(shape.shape)] * 6,
        ),
        out_shape=[shape] * 6,
        compiler_params=params(32),
        cost_estimate=cost(3 * down.size, 12 * down.size),
        name="split",
    )(bits, down, up, out)


def combine_kernel(last, bit_ref, *refs):
    count = len(refs) // (3 if last else 4)
    for part in range(count):
        keep, got, outs = refs[2 * part], refs[2 * part + 1], refs[2 * count :]
        total = lambda rows: (keep[rows].astype(F32) + got[rows].astype(F32)).astype(BF16)
        if last:
            outs[part][...] = total(slice(None))
        else:
            half = keep.shape[0] // 2
            bit = bit_ref[part]
            outs[2 * part][...] = total(pl.ds(bit * half, half))
            outs[2 * part + 1][...] = total(pl.ds((1 - bit) * half, half))


def combine(bits, keeps, gots, last):
    operands = [a for pair in zip(keeps, gots) for a in pair]
    shapes = []
    for keep in keeps:
        n, rows, columns = keep.shape
        shapes += [jax.ShapeDtypeStruct(keep.shape, BF16)] if last else [jax.ShapeDtypeStruct((n // 2, rows, columns), BF16)] * 2
    size = sum(k.size for k in keeps)
    outs = pl.pallas_call(
        lambda *refs: combine_kernel(last, *refs),
        grid_spec=pltpu.PrefetchScalarGridSpec(
            num_scalar_prefetch=1,
            grid=(1,),
            in_specs=[whole(a.shape) for a in operands],
            out_specs=[whole(s.shape) for s in shapes],
        ),
        out_shape=shapes,
        compiler_params=params(32),
        cost_estimate=cost(2 * size, 6 * size),
        name="combine",
    )(bits, *operands)
    return (outs, None) if last else (outs[::2], outs[1::2])


def join_kernel(bit_ref, *refs):
    count = len(refs) // 3
    for part in range(count):
        mine, got, out = refs[2 * part], refs[2 * part + 1], refs[2 * count + part]
        size = mine.shape[0]
        bit = bit_ref[part]
        out[pl.ds(bit * size, size)] = mine[...]
        out[pl.ds((1 - bit) * size, size)] = got[...]


def join(bits, mines, gots):
    operands = [a for pair in zip(mines, gots) for a in pair]
    shapes = [jax.ShapeDtypeStruct((2 * m.shape[0],) + m.shape[1:], BF16) for m in mines]
    size = sum(m.size for m in mines)
    return pl.pallas_call(
        join_kernel,
        grid_spec=pltpu.PrefetchScalarGridSpec(
            num_scalar_prefetch=1,
            grid=(1,),
            in_specs=[whole(a.shape) for a in operands],
            out_specs=[whole(s.shape) for s in shapes],
        ),
        out_shape=shapes,
        compiler_params=params(32),
        cost_estimate=cost(size, 8 * size),
        name="join",
    )(bits, *operands)


def step_bits(orders, step):
    return jnp.stack([bit_of(*order[step]) for order in orders]).astype(jnp.int32)


def send_all(values, orders, step):
    return [swap(value, *order[step]) for value, order in zip(values, orders)]


def tie(*values):
    return lax.optimization_barrier(values)


def sum_all(value, order):
    for axis, bit in order:
        value = value + swap(value, axis, bit)
    return value


def finish_kernel(first, info_ref, a_ref, b_ref, c_ref, *refs):
    down_ref, up_ref, out_ref = refs[-3:]
    main, width = a_ref.shape
    rows = down_ref.shape[0]
    tail = rows - main
    wide = lambda value: value.astype(F32)
    down_ref[:main, :] = wide(a_ref[...])
    down_ref[main:, :] = wide(c_ref[:tail, :])
    for panel in range(rows // width):
        begin, end = panel * width, (panel + 1) * width
        columns = slice(begin, end)
        inner = min(end, main) - begin
        up_ref[:inner, columns] = wide(b_ref[begin : begin + inner, :])
        if inner < width:
            up_ref[inner:, columns] = wide(c_ref[tail : tail + width - inner, :])
    out_ref[...] = wide(c_ref[2 * tail :, :])


def finish(side, parts, hidden, carried=None):
    width = parts[0].shape[1]
    rows = hidden // 2
    shapes = [(hidden, width), (width, hidden), (width, width)]
    specs = [
        pl.BlockSpec((rows, width), lambda i, info: (info[0], 0)),
        pl.BlockSpec((width, rows), lambda i, info: (0, info[0])),
        pl.BlockSpec((width // 2, width), lambda i, info: (info[0], 0)),
    ]
    carried = carried or []
    return pl.pallas_call(
        lambda *refs: finish_kernel(not carried, *refs),
        grid_spec=pltpu.PrefetchScalarGridSpec(
            num_scalar_prefetch=1,
            grid=(1,),
            in_specs=[whole(p.shape) for p in parts] + [pl.BlockSpec(memory_space=pl.ANY)] * len(carried),
            out_specs=specs,
        ),
        out_shape=[jax.ShapeDtypeStruct(s, F32) for s in shapes],
        input_output_aliases={4 + i: i for i in range(len(carried))},
        compiler_params=params(48),
        cost_estimate=cost(3 * rows * width, 12 * rows * width),
        name="finish",
    )(side, *parts, *carried)


def finish_heads_kernel(info_ref, *refs):
    count = (len(refs) - 3) // 2
    for side in range(2):
        base = (info_ref[0] if side == 0 else 1 - info_ref[0]) * count * PAIR
        for pair in range(count):
            source = refs[side * count + pair]
            for part in range(3):
                columns = pl.ds(pl.multiple_of(base + pair * PAIR, PAIR), PAIR)
                refs[2 * count + part][:, columns] = source[:, part * PAIR : (part + 1) * PAIR].astype(F32)


def finish_heads(side, own, there):
    rows = own[0].shape[0]
    width = 2 * len(own) * PAIR
    step = rows // 4
    return pl.pallas_call(
        finish_heads_kernel,
        grid_spec=pltpu.PrefetchScalarGridSpec(
            num_scalar_prefetch=1,
            grid=(rows // step,),
            in_specs=[pl.BlockSpec((step, 3 * PAIR), lambda i, _: (i, 0))] * (2 * len(own)),
            out_specs=[pl.BlockSpec((step, width), lambda i, _: (i, 0))] * 3,
        ),
        out_shape=[jax.ShapeDtypeStruct((rows, width), F32)] * 3,
        compiler_params=params(32),
        cost_estimate=cost(3 * rows * width, 18 * rows * width),
        name="finish_heads",
    )(side, *own, *there)


def local(
    hidden_in,
    seg_lengths,
    query_weight,
    query_bias,
    key_weight,
    value_weight,
    value_bias,
    out_weight,
    out_bias,
    first_gain,
    first_shift,
    up_weight,
    up_bias,
    down_weight,
    down_bias,
    second_gain,
    second_shift,
    cot_out,
    cot_pool,
):
    _, chunk, width = hidden_in.shape
    length = 4 * chunk
    half = width // 2
    hidden_units = up_weight.shape[1]
    dp_order = [("dp", 1 << i) for i in range((lax.axis_size("dp") - 1).bit_length())]
    far, near = ("seq", 2), ("seq", 1)
    high, low = bit_of(*far), bit_of(*near)
    mine = lax.axis_index("seq")
    whole_number = lambda values: jnp.stack([jnp.asarray(v, jnp.int32) for v in values])

    pick = lambda array, i: lax.dynamic_index_in_dim(array, i, 0, keepdims=False)
    own = pick(hidden_in, high)
    came = swap(pick(hidden_in, 1 - high), *far)
    own_there = swap(own, *near)
    came_there = swap(came, *near)
    cot_own = pick(cot_out, high)
    cot_came = swap(pick(cot_out, 1 - high), *far)

    lengths = pick(seg_lengths, high)
    ends = jnp.cumsum(lengths)
    begins = ends - lengths
    sizes = lengths[:NSENT].astype(F32)
    origin = jnp.min(jnp.where(lengths == LONGEST, begins, length))
    inside = lambda t, lo, hi: (t[:, None] >= lo[None, :]) & (t[:, None] < hi[None, :])
    lanes = lambda m: jnp.pad(m, ((0, 0), (0, PAIR - SLOTS)))
    positions = jnp.arange(length, dtype=jnp.int32)
    member = lanes(inside(positions, begins, ends)).astype(BF16)
    turned = (begins - origin) % length
    turned_ends = turned + lengths
    held = lanes(inside(positions, turned, turned_ends))
    query_feature = held.astype(BF16)
    key_feature = jnp.where(held, 0.0, MASKED).astype(BF16)
    block_first = jnp.arange(length // QB, dtype=jnp.int32) * QB
    lowest = jnp.sum(jnp.where(inside(block_first, turned, turned_ends), turned[None, :], 0), axis=1)
    highest = jnp.sum(jnp.where(inside(block_first + QB - 1, turned, turned_ends), turned_ends[None, :], 0), axis=1)
    per = KB // GRAIN
    starts = lowest // GRAIN
    counts = ((highest + GRAIN - 1) // GRAIN - starts + per - 1) // per
    starts = jnp.minimum(starts, length // GRAIN - counts * per)
    ranges = jnp.concatenate([origin[None], starts, counts, low[None]]).astype(jnp.int32)
    turn = whole_number([origin, low])

    take = lambda weight: lax.dynamic_slice_in_dim(weight, low * half, half, 1)
    by_pair = lambda arrays: jnp.concatenate(
        [a[:, g : g + PAIR] for g in range(0, half, PAIR) for a in arrays], axis=1
    )
    vector = lambda bias: lax.dynamic_slice_in_dim(bias, low * half, half, 0)[None, :]
    packed_weight = by_pair([take(query_weight), take(key_weight), take(value_weight)])
    packed_bias = by_pair([vector(query_bias), jnp.zeros((1, half), F32), vector(value_bias)])
    scale = by_pair([jnp.full((1, half), 0.125, F32)] + [jnp.ones((1, half), F32)] * 2)

    places = whole_number([origin, mine, mine ^ 2, mine ^ 1, mine ^ 3])
    rolled_input, packed = project(places, (own, came, own_there, came_there), packed_weight, packed_bias, scale)
    rolled_heads, att_mine, att_send, lse = attend(ranges, packed, query_feature, key_feature)
    att_other = swap(att_send, *near)

    out_mine = lax.dynamic_slice_in_dim(out_weight, low * half, half, 0)
    out_other = lax.dynamic_slice_in_dim(out_weight, (1 - low) * half, half, 0)
    pool_weight = jnp.pad(pick(cot_pool, high) / sizes[:, None], ((0, PAIR - NSENT), (0, 0)))
    pool_upper = pool_weight.astype(BF16)
    pool_weight = jnp.concatenate([pool_upper, (pool_weight - pool_upper.astype(F32)).astype(BF16)], axis=0)
    vectors = jnp.stack([out_bias, first_gain, first_shift, down_bias, second_gain, second_shift])
    token_info = whole_number([high, low, low + 2])
    (
        final, act, branch, normed, pre, attn, d_first, d_att_mine, d_att_send, pool_part, small_part, up_small,
    ) = token_layers(
        token_info, att_mine, att_other, own, came, cot_own, cot_came, member, pool_weight,
        out_mine, out_other, up_weight, down_weight, vectors, up_bias[None, :],
    )
    d_att_other = swap(d_att_send, *near)

    orders = ([far] + dp_order, dp_order[:1] + [far] + dp_order[1:], dp_order[1:] + dp_order[:1] + [far])
    steps = len(orders[0])
    bits = [step_bits(orders, i) for i in range(steps)]
    pieces_of = lambda part: part.reshape((1 << (steps - 1), -1, part.shape[-1]))
    here, over = whole_number([low]), whole_number([1 - low])

    send_down = product(over, act, branch)
    down_there = swap(send_down, *near)
    send_up = product(over, *tie(normed, pre, send_down)[:2])
    up_there = swap(send_up, *near)
    send_out = head_product(*tie(att_other, attn, send_up)[:2])
    out_there = swap(send_out, *near)
    own_out_left, own_attn, _ = tie(att_mine, attn, send_out)
    down_left, down_right, down_there, _ = tie(act, branch, down_there, send_out)
    grad_part_down = product(here, down_left, down_right, down_there)
    up_left, up_right, up_there, _ = tie(normed, pre, up_there, grad_part_down)
    grad_part_up = product(here, up_left, up_right, up_there)
    own_out_left, own_attn, out_there, _ = tie(own_out_left, own_attn, out_there, grad_part_up)
    grad_part_out = head_product(own_out_left, own_attn, out_there)
    stays_and_goes = split(bits[0], grad_part_down, grad_part_up, grad_part_out)
    keeps, sends = [pieces_of(p) for p in stays_and_goes[::2]], [pieces_of(p) for p in stays_and_goes[1::2]]

    class Chain:
        def __init__(self, keeps, sends):
            self.keeps, self.sends, self.step, self.down = keeps, sends, 0, True

        def advance(self, *work):
            gots = send_all(self.sends, orders, self.step)
            gots = tie(*gots, *work)[: len(gots)]
            if self.down:
                self.step += 1
                last = self.step == steps
                out = combine(bits[min(self.step, steps - 1)], self.keeps, gots, last)
                self.keeps, self.sends = out
                if last:
                    self.down, self.step, self.sends = False, steps - 1, self.keeps
            else:
                self.sends = join(bits[self.step], self.sends, gots)
                self.step -= 1

        def before(self, *values):
            out = tie(*values, *self.sends)
            self.sends = list(out[len(values) :])
            return out[: len(values)]

    chain = Chain(keeps, sends)
    d_mine, d_other = chain.before(d_att_mine, d_att_other)
    d_heads, delta = roll_back(turn, d_mine, d_other, rolled_heads)
    d_rest = rest_back(ranges, packed, d_heads, lse, delta, query_feature, key_feature)
    chain.advance(d_rest)
    d_long = []
    for g in range(half // PAIR):
        (heads_in,) = chain.before(d_heads)
        d_long.append(long_back(g, packed, heads_in, lse, delta))
        if g > 0:
            chain.advance(d_long[-1])
    (rest_in,) = chain.before(d_rest)
    *head_parts, d_packed_bias = packed_product(bits[0], rolled_input, d_long, rest_in)
    chain.advance(head_parts[0])
    head_chain = Chain([pieces_of(p) for p in head_parts[::2]], [pieces_of(p) for p in head_parts[1::2]])
    (rest_in,) = head_chain.before(*chain.before(d_rest))
    d_keep, d_send = input_grad(turn, d_long, rest_in, packed_weight)
    d_got = swap(d_send, *near)
    chain.advance(d_keep)
    head_chain.advance(d_keep)
    (d_got,) = head_chain.before(*chain.before(d_got))
    d_inputs = (d_first + d_keep.astype(F32) + d_got.astype(F32)).reshape(2, chunk, width)

    def to_rows(array):
        keep = pick(array, high)
        other = swap(pick(array, 1 - high).astype(BF16), *far).astype(array.dtype)
        return jnp.stack([jnp.where(high == 0, keep, other), jnp.where(high == 0, other, keep)])

    layer_out = to_rows(final.reshape(2, chunk, width))
    grad_hidden = to_rows(d_inputs)

    pool_part = pool_part[:NSENT]
    pool_row = (pool_part + swap(pool_part, *near)) / sizes[:, None]
    pool_far = swap(pool_row, *far)
    pooled = jnp.stack([jnp.where(high == 0, pool_row, pool_far), jnp.where(high == 0, pool_far, pool_row)])

    while chain.step >= 0 or head_chain.step >= 0:
        if chain.step >= 0:
            chain.advance()
        if head_chain.step >= 0:
            head_chain.advance()

    flat = lambda part: part.reshape(-1, part.shape[-1])
    parts = [flat(p) for p in chain.sends]
    there = [swap(p, *near) for p in parts]
    grad_down, grad_up, grad_out = finish(over, there, hidden_units, finish(here, parts, hidden_units))
    parts = [flat(p) for p in head_chain.sends]
    there = [swap(p, *near) for p in parts]
    head_grads = finish_heads(here, parts, there)

    d_packed_bias = d_packed_bias.reshape(half // PAIR, 3, PAIR)
    first_core = low == 0
    spread = lambda part: jnp.where(
        first_core, jnp.concatenate([part, jnp.zeros_like(part)]), jnp.concatenate([jnp.zeros_like(part), part])
    )[None, :]
    small = jnp.concatenate(
        [spread(d_packed_bias[:, 0].reshape(-1)), spread(d_packed_bias[:, 2].reshape(-1)), small_part[:6], up_small.reshape(-1, width)],
        axis=0,
    )
    small = sum_all(small, [near, far] + dp_order)
    return (
        layer_out,
        pooled,
        grad_hidden,
        head_grads[0],
        small[0],
        head_grads[1],
        head_grads[2],
        small[1],
        grad_out,
        small[2],
        small[3],
        small[4],
        grad_up,
        small[8:].reshape(-1),
        grad_down,
        small[5],
        small[6],
        small[7],
    )


def solution(mesh):
    tokens, rows = P("dp", "seq", None), P("dp", None)
    pool = P("dp", None, None)
    return jax.shard_map(
        local,
        mesh=mesh,
        in_specs=(tokens, rows) + (P(),) * 15 + (tokens, pool),
        out_specs=(tokens, pool, tokens) + (P(),) * 15,
        check_vma=False,
    )
```

time: 687 us -> 439 us (0.64)
  matrix products: 103 us -> 0 us
  waiting for transfers between devices: 192 us -> 109 us
  other arithmetic: 74.9 us -> 16.6 us
  local copies, waits for them, and re-layouts: 32.3 us -> 51.3 us
  starting transfers between devices: 85.4 us -> 68.9 us
  Pallas kernels: 192 us -> 182 us
    dot_general x16 -> x0, matrix products: 103 us -> none  [the longest x14 98.4 us: dot(): lax.dot_general(left, right, (contract, ((), ())), preferred_element_type...]
    ppermute x87 -> x73, waiting for transfers between devices: 192 us -> 109 us  [swap(): return lax.ppermute(value, axis, [(i, i ^ bit) for i in range(size)])]
    pallas_call x1, Pallas kernels: 84.8 us -> 23.7 us  [attend(): pl.pallas_call(attend_kernel, grid_spec=pltpu.PrefetchScalarGridSpec(num_...]
    pallas_call x2 -> x35, Pallas kernels: 107 us -> 159 us  [the longest x1 40.1 us: token_layers(): pl.pallas_call(tokens_kernel, grid_spec=pltpu.PrefetchScalarGridSpec(num_...]
    unnamed x115 -> x159, local copies, waits for them, and re-layouts: 8.71 us -> 37.6 us
    select_n x39 -> x2, other arithmetic: 26.9 us -> 0.01 us  [local(): jnp.where(first_core, jnp.concatenate([part, jnp.zeros_like(part)]), jnp....]
    convert_element_type x42 -> x4, other arithmetic: 25.8 us -> 1.95 us  [the longest x1 0.95 us: local(): member = lanes(inside(positions, begins, ends)).astype(BF16)]
    ppermute x87 -> x73, starting transfers between devices: 85.4 us -> 68.9 us  [swap(): return lax.ppermute(value, axis, [(i, i ^ bit) for i in range(size)])]
  transfers between devices with their start and end apart: 87 -> 73, of which waited for: 54 -> 26; matrix products, arithmetic and copies ran while one was open for 13% -> 8% of each run, Pallas kernels for 28% -> 26%
where the time goes in v2:
time: 439 us; the launch traced here: 431 us
  Pallas kernels  182 us (41%)
  waiting for transfers between devices  109 us (25%)
  starting transfers between devices  68.9 us (16%)
  local copies, waits for them, and re-layouts  51.3 us (12%)
  other arithmetic  16.6 us (4%)
    ppermute x73, waiting for transfers between devices, swap(): return lax.ppermute(value, axis, [(i, i ^ bit) for i in range(size)])  109 us
    ppermute x73, starting transfers between devices, swap(): return lax.ppermute(value, axis, [(i, i ^ bit) for i in range(size)])  68.9 us
    pallas_call x1, Pallas kernels, token_layers(): pl.pallas_call(tokens_kernel, grid_spec=pltpu.PrefetchScalarGridSpec(num_...  40.1 us
    unnamed x159, local copies, waits for them, and re-layouts  37.6 us
    pallas_call x3, Pallas kernels, long_back(): pl.pallas_call(long_back_kernel, grid=(1,), in_specs=[at(LONGEST, 3 * PAI...  23.9 us
    pallas_call x1, Pallas kernels, attend(): pl.pallas_call(attend_kernel, grid_spec=pltpu.PrefetchScalarGridSpec(num_...  23.7 us
    pallas_call x4, Pallas kernels, product(): pl.pallas_call(lambda *refs: product_kernel(bool(extra), *refs), grid_spe...  17.3 us
    pallas_call x1, Pallas kernels, rest_back(): pl.pallas_call(rest_back_kernel, grid_spec=pltpu.PrefetchScalarGridSpec(n...  14.3 us
  transfers between devices with their start and end apart: 73, of which 26 were waited for; matrix products, arithmetic and copies ran while one was open for 8% of the time, Pallas kernels for 26%

profile of v2, /device:TPU:0, one launch (start us, length us, event | category | flops | bytes accessed | tf_op | source)
XLA Modules:
  0.0 430.8 jit_solution(15763350474431230687)
XLA Ops:
  28.5 9.3 %project.1 = (bf16[2048,768]{1,0:T(8,128)(2,1)S(1)}, bf16[2048,1152]{1,0:T(8,128)(2,1)S(1)}) custom-call(s32[5]{0:T(128)S(1)} %stack.123.info_ref, bf16[512,768]{1,0:T(8,128)(2,1)S(1)} %get-tuple-element.515.a_ref.xa_ref, bf16[512,768]{1,0:T(8,128)(2,1)S(1)} %collective-permute-done.b_ref.xb_ref, bf16[512,768]{1,0:T(8,128)(2,1)} %collective-permute-done.1.c_ref, ...), custom_call_target="tpu_custom_call" | custom-call | flops 4429185024 | bytes 22020096 | tf_op jit(solution)/shard_map/project/pallas_call | solution.py:83
  41.7 23.7 %attend.1 = (bf16[2048,384]{1,0:T(8,128)(2,1)S(1)}, bf16[1024,384]{1,0:T(8,128)(2,1)S(1)}, bf16[1024,384]{1,0:T(8,128)(2,1)S(1)}, f32[8,1536]{1,0:T(8,128)S(1)}) custom-call(s32[18]{0:T(128)S(1)} %pad_add_fusion.1.info_ref, bf16[2048,1152]{1,0:T(8,128)(2,1)} %copy-done.47, bf16[2048,128]{1,0:T(8,128)(2,1)S(1)} %pad_convert_fusion.1.qf_ref, ...), custom_call_target="tpu_custom_call" | custom-call | flops 9663676416 | bytes 9437184 | tf_op jit(solution)/shard_map/attend/pallas_call | solution.py:230
  70.6 40.1 %token_layers.1 = (bf16[1024,768]{1,0:T(8,128)(2,1)}, bf16[1024,3072]{1,0:T(8,128)(2,1)}, bf16[1024,768]{1,0:T(8,128)(2,1)}, bf16[1024,768]{1,0:T(8,128)(2,1)}, ...) custom-call(s32[3]{0:T(128)} %pad_add_fusion.info_ref, ...), custom_call_target="tpu_custom_call" | custom-call | flops 21743271936 | bytes 50331648 | tf_op jit(solution)/shard_map/token_layers/pallas_call | solution.py:573
  114.9 4.1 product.4
  119.4 4.2 product.5
  131.9 4.6 %product.6.down_ref = bf16[1536,768]{1,0:T(8,128)(2,1)S(1)} custom-call(s32[1]{0:T(128)} %bitcast.1.refs_0_.info_ref, bf16[1024,3072]{1,0:T(8,128)(2,1)S(1)} %copy-done.4, bf16[1024,768]{1,0:T(8,128)(2,1)S(1)} %copy-done.8, bf16[1536,768]{1,0:T(8,128)(2,1)} %collective-permute-done.9.refs_3_), custom_call_target="tpu_custom_call" | custom-call | flops 2415919104 | bytes 4718592 | tf_op jit(solution)/shard_map/product/pallas_call | solution.py:605
  136.6 4.4 %product.7.up_ref = bf16[1536,768]{1,0:T(8,128)(2,1)S(1)} custom-call(s32[1]{0:T(128)} %bitcast.1.refs_0_.info_ref, bf16[1024,768]{1,0:T(8,128)(2,1)S(1)} %copy-done.6, bf16[1024,3072]{1,0:T(8,128)(2,1)S(1)} %bitcast.97, bf16[1536,768]{1,0:T(8,128)(2,1)} %collective-permute-done.10.refs_3_), custom_call_target="tpu_custom_call" | custom-call | flops 2415919104 | bytes 4718592 | tf_op jit(solution)/shard_map/product/pallas_call | solution.py:605
  152.7 14.3 %rest_back.1.refs_3_ = bf16[1024,1152]{1,0:T(8,128)(2,1)S(1)} custom-call(s32[18]{0:T(128)S(1)} %pad_add_fusion.1.info_ref, bf16[2048,1152]{1,0:T(8,128)(2,1)S(1)} %copy-done.48, bf16[2048,384]{1,0:T(8,128)(2,1)S(1)} %get-tuple-element.294.up_ref, f32[8,1536]{1,0:T(8,128)S(1)} %get-tuple-element.267.lse_ref, f32[8,1536]{1,0:T(8,128)S(1)} %get-tuple-element.268.delta_ref, ...), custom_call_target="tpu_custom_call" | custom-call | flops 9663676416 | bytes 6291456 | tf_op jit(solution)/shard_map/rest_back/pallas_call | solution.py:396
  168.8 7.9 %long_back.4.refs_1_ = bf16[1024,384]{1,0:T(8,128)(2,1)S(1)} custom-call(bf16[2048,1152]{1,0:T(8,128)(2,1)S(1)} %copy-done.48, bf16[2048,384]{1,0:T(8,128)(2,1)S(1)} %get-tuple-element.294.up_ref, f32[8,1536]{1,0:T(8,128)S(1)} %get-tuple-element.267.lse_ref, f32[8,1536]{1,0:T(8,128)S(1)} %get-tuple-element.268.delta_ref), custom_call_target="tpu_custom_call" | custom-call | flops 5368709120 | bytes 2097152 | tf_op jit(solution)/shard_map/long_back/pallas_call | solution.py:328
  181.0 8.1 %long_back.3.refs_0_ = bf16[1024,384]{1,0:T(8,128)(2,1)S(1)} custom-call(bf16[2048,1152]{1,0:T(8,128)(2,1)S(1)} %copy-done.48, bf16[2048,384]{1,0:T(8,128)(2,1)S(1)} %get-tuple-element.294.up_ref, f32[8,1536]{1,0:T(8,128)S(1)} %get-tuple-element.267.lse_ref, f32[8,1536]{1,0:T(8,128)S(1)} %get-tuple-element.268.delta_ref), custom_call_target="tpu_custom_call" | custom-call | flops 5368709120 | bytes 2097152 | tf_op jit(solution)/shard_map/long_back/pallas_call | solution.py:328
  189.2 10.8 %collective-permute-done.17.refs_6_ = bf16[4,72,768]{2,1,0:T(8,128)(2,1)S(1)} collective-permute-done((bf16[4,72,768]{2,1,0:T(8,128)(2,1)S(1)}, bf16[4,72,768]{2,1,0:T(8,128)(2,1)S(1)}, u32[]{:S(2)}, u32[]{:S(2)}) %collective-permute-start.17) | collective-permute-done | bytes 442400 | tf_op jit(solution)/shard_map/ppermute | solution.py:28
  203.4 7.9 %long_back.5.refs_2_ = bf16[1024,384]{1,0:T(8,128)(2,1)S(1)} custom-call(bf16[2048,1152]{1,0:T(8,128)(2,1)S(1)} %copy-done.48, bf16[2048,384]{1,0:T(8,128)(2,1)S(1)} %get-tuple-element.294.up_ref, f32[8,1536]{1,0:T(8,128)S(1)} %get-tuple-element.267.lse_ref, f32[8,1536]{1,0:T(8,128)S(1)} %get-tuple-element.268.delta_ref), custom_call_target="tpu_custom_call" | custom-call | flops 5368709120 | bytes 2097152 | tf_op jit(solution)/shard_map/long_back/pallas_call | solution.py:328
  218.3 5.6 %packed_product.1 = (bf16[384,384]{1,0:T(8,128)(2,1)S(1)}, bf16[384,384]{1,0:T(8,128)(2,1)S(1)}, bf16[384,384]{1,0:T(8,128)(2,1)S(1)}, bf16[384,384]{1,0:T(8,128...) custom-call(s32[3]{0:T(128)S(1)} %pad_add_fusion.3.bit_ref, ...), custom_call_target="tpu_custom_call" | custom-call | flops 3623878656 | bytes 12582912 | tf_op jit(solution)/shard_map/packed_product/pallas_call | solution.py:662
  227.0 9.5 %input_grad.1 = (bf16[1024,768]{1,0:T(8,128)(2,1)S(1)}, bf16[1024,768]{1,0:T(8,128)(2,1)S(1)}) custom-call(s32[2]{0:T(128)S(1)} %pad_add_fusion.2.info_ref, bf16[1024,384]{1,0:T(8,128)(2,1)S(1)} %long_back.3.refs_0_, bf16[1024,384]{1,0:T(8,128)(2,1)S(1)} %long_back.4.refs_1_, bf16[1024,384]{1,0:T(8,128)(2,1)S(1)} %long_back.5.refs_2_, ...), custom_call_target="tpu_custom_call" | custom-call | flops 4429185024 | bytes 12582912 | tf_op jit(solution)/shard_map/input_grad/pallas_call | solution.py:451
  245.5 7.9 %collective-permute-done.26.refs_3_ = bf16[1,72,768]{2,1,0:T(8,128)(2,1)S(1)} collective-permute-done((bf16[1,72,768]{2,1,0:T(8,128)(2,1)S(1)}, bf16[1,72,768]{2,1,0:T(8,128)(2,1)S(1)}, u32[]{:S(2)}, u32[]{:S(2)}) %collective-permute-start.26) | collective-permute-done | bytes 110624 | tf_op jit(solution)/shard_map/ppermute | solution.py:28
  269.8 5.7 %collective-permute-done.34.refs_6_ = bf16[4,48,384]{2,1,0:T(8,128)(2,1)} collective-permute-done((bf16[4,48,384]{2,1,0:T(8,128)(2,1)}, bf16[4,48,384]{2,1,0:T(8,128)(2,1)}, u32[]{:S(2)}, u32[]{:S(2)}) %collective-permute-start.34) | collective-permute-done | bytes 147488 | tf_op jit(solution)/shard_map/ppermute | solution.py:28
  297.5 11.7 %collective-permute-done.41.refs_1_ = bf16[1,48,384]{2,1,0:T(8,128)(2,1)S(1)} collective-permute-done((bf16[1,48,384]{2,1,0:T(8,128)(2,1)S(1)}, bf16[1,48,384]{2,1,0:T(8,128)(2,1)S(1)}, u32[]{:S(2)}, u32[]{:S(2)}) %collective-permute-start.41) | collective-permute-done | bytes 36896 | tf_op jit(solution)/shard_map/ppermute | solution.py:28
  329.9 16.8 %collective-permute-done.47.refs_1_ = bf16[4,48,384]{2,1,0:T(8,128)(2,1)S(1)} collective-permute-done((bf16[4,48,384]{2,1,0:T(8,128)(2,1)S(1)}, bf16[4,48,384]{2,1,0:T(8,128)(2,1)S(1)}, u32[]{:S(2)}, u32[]{:S(2)}) %collective-permute-start.47) | collective-permute-done | bytes 147488 | tf_op jit(solution)/shard_map/ppermute | solution.py:28
  348.2 11.1 %collective-permute-done.48.refs_3_ = bf16[4,48,384]{2,1,0:T(8,128)(2,1)S(1)} collective-permute-done((bf16[4,48,384]{2,1,0:T(8,128)(2,1)S(1)}, bf16[4,48,384]{2,1,0:T(8,128)(2,1)S(1)}, u32[]{:S(2)}, u32[]{:S(2)}) %collective-permute-start.48) | collective-permute-done | bytes 147488 | tf_op jit(solution)/shard_map/ppermute | solution.py:28
  360.6 7.3 %collective-permute-done.49.refs_5_ = bf16[4,48,384]{2,1,0:T(8,128)(2,1)S(1)} collective-permute-done((bf16[4,48,384]{2,1,0:T(8,128)(2,1)S(1)}, bf16[4,48,384]{2,1,0:T(8,128)(2,1)S(1)}, u32[]{:S(2)}, u32[]{:S(2)}) %collective-permute-start.49) | collective-permute-done | bytes 147488 | tf_op jit(solution)/shard_map/ppermute | solution.py:28
  398.4 9.2 %collective-permute-done.31 = bf16[512,768]{1,0:T(8,128)(2,1)} collective-permute-done((bf16[512,768]{1,0:T(8,128)(2,1)}, bf16[512,768]{1,0:T(8,128)(2,1)}, u32[]{:S(2)}, u32[]{:S(2)}) %collective-permute-start.31) | collective-permute-done | bytes 786464 | tf_op jit(solution)/shard_map/ppermute | solution.py:28
  412.6 4.5 %finish_heads.1 = (f32[768,768]{1,0:T(8,128)}, f32[768,768]{1,0:T(8,128)}, f32[768,768]{1,0:T(8,128)}) custom-call(s32[1]{0:T(128)} %bitcast.1.refs_0_.info_ref, bf16[768,384]{1,0:T(8,128)(2,1)S(1)} %bitcast.102, bf16[768,384]{1,0:T(8,128)(2,1)S(1)} %bitcast.104, bf16[768,384]{1,0:T(8,128)(2,1)S(1)} %bitcast.106, ...), custom_call_target="tpu_custom_call" | custom-call | flops 1769472 | bytes 10616832 | tf_op jit(solution)/shard_map/finish_heads/pallas_call | solution.py:854
  417.1 6.8 %finish.2 = (f32[3072,768]{1,0:T(8,128)}, f32[768,3072]{1,0:T(8,128)}, f32[768,768]{1,0:T(8,128)}) custom-call(s32[1]{0:T(128)} %bitcast.1.refs_0_.info_ref, bf16[1152,768]{1,0:T(8,128)(2,1)} %bitcast.51.refs_1_, bf16[1152,768]{1,0:T(8,128)(2,1)} %bitcast.52.refs_2_, bf16[1152,768]{1,0:T(8,128)(2,1)} %bitcast.53.refs_3_), custom_call_target="tpu_custom_call" | custom-call | flops 3538944 | bytes 14155776 | tf_op jit(solution)/shard_map/finish/pallas_call | solution.py:823
  424.0 6.3 %finish.3 = (f32[3072,768]{1,0:T(8,128)}, f32[768,3072]{1,0:T(8,128)}, f32[768,768]{1,0:T(8,128)}) custom-call(s32[1]{0:T(128)} %bitcast.29.refs_0_, bf16[1152,768]{1,0:T(8,128)(2,1)S(1)} %collective-permute-done.70.refs_1_, bf16[1152,768]{1,0:T(8,128)(2,1)} %collective-permute-done.71.refs_2_, ...), custom_call_target="tpu_custom_call", output_to_operand_aliasing={{0}: (4, {}), {1}: (5, {}), {2}: (6, {})} | custom-call | flops 3538944 | bytes 14155776 | tf_op jit(solution)/shard_map/finish/pallas_call | solution.py:823
  (391 shorter events, 186.5 us)
Async XLA Ops:
  3.2 22.9 %collective-permute-start = (bf16[512,768]{1,0:T(8,128)(2,1)}, bf16[512,768]{1,0:T(8,128)(2,1)S(1)}, u32[]{:S(2)}, u32[]{:S(2)}) collective-permute-start(bf16[512,768]{1,0:T(8,128)(2,1)} %get-tuple-element.514), channel_id=1, source_target_pairs={{0,2},{1,3},{2,0},{3,1},{4,6},{5,7},{6,4},{7,5},{8,10},{9,11},{10,... | collective-permute-start | bytes 2359304 | tf_op jit(solution)/shard_map/ppermute | solution.py:28
  6.1 21.5 %collective-permute-start.1 = (bf16[512,768]{1,0:T(8,128)(2,1)S(1)}, bf16[512,768]{1,0:T(8,128)(2,1)}, u32[]{:S(2)}, u32[]{:S(2)}) collective-permute-start(bf16[512,768]{1,0:T(8,128)(2,1)S(1)} %get-tuple-element.515.a_ref.xa_ref), channel_id=1, source_target_pairs={{0,1},{1,0},{2,3},{3,2},{4,5},{5,4},{6,7},{7,6},{8,9},{9,8},{10,11... | collective-permute-start | bytes 2359304 | tf_op jit(solution)/shard_map/ppermute | solution.py:28
  7.4 62.2 %collective-permute-start.4 = (bf16[512,768]{1,0:T(8,128)(2,1)}, bf16[512,768]{1,0:T(8,128)(2,1)}, u32[]{:S(2)}, u32[]{:S(2)}) collective-permute-start(bf16[512,768]{1,0:T(8,128)(2,1)} %get-tuple-element.512), channel_id=1, source_target_pairs={{0,2},{1,3},{2,0},{3,1},{4,6},{5,7},{6,4},{7,5},{8,10},{9,11},{10,... | collective-permute-start | bytes 2359304 | tf_op jit(solution)/shard_map/ppermute | solution.py:28
  124.5 18.4 %collective-permute-start.8 = (bf16[1024,384]{1,0:T(8,128)(2,1)}, bf16[1024,384]{1,0:T(8,128)(2,1)}, u32[]{:S(2)}, u32[]{:S(2)}) collective-permute-start(bf16[1024,384]{1,0:T(8,128)(2,1)} %get-tuple-element.235), channel_id=1, source_target_pairs={{0,1},{1,0},{2,3},{3,2},{4,5},{5,4},{6,7},{7,6},{8,9},{9,8},{10,11... | collective-permute-start | bytes 2359304 | tf_op jit(solution)/shard_map/ppermute | solution.py:28
  142.9 24.0 %collective-permute-start.12 = (bf16[8,72,768]{2,1,0:T(8,128)(2,1)S(1)}, bf16[8,72,768]{2,1,0:T(8,128)(2,1)S(1)}, u32[]{:S(2)}, u32[]{:S(2)}) collective-permute-start(bf16[8,72,768]{2,1,0:T(8,128)(2,1)S(1)} %bitcast.112), channel_id=1, source_target_pairs={{0,2},{1,3},{2,0},{3,1},{4,6},{5,7},{6,4},{7,5},{8,10},{9,11},{10,... | collective-permute-start | bytes 2654216 | tf_op jit(solution)/shard_map/ppermute | solution.py:28
  144.0 23.0 %collective-permute-start.13 = (bf16[8,72,768]{2,1,0:T(8,128)(2,1)S(1)}, bf16[8,72,768]{2,1,0:T(8,128)(2,1)S(1)}, u32[]{:S(2)}, u32[]{:S(2)}) collective-permute-start(bf16[8,72,768]{2,1,0:T(8,128)(2,1)S(1)} %bitcast.111), channel_id=1, source_target_pairs={{0,4},{4,0},{8,12},{12,8},{16,20},{20,16},{24,28},{28,24},{1,5},{5... | collective-permute-start | bytes 2654216 | tf_op jit(solution)/shard_map/ppermute | solution.py:28
  146.4 21.2 %collective-permute-start.14 = (bf16[8,72,768]{2,1,0:T(8,128)(2,1)S(1)}, bf16[8,72,768]{2,1,0:T(8,128)(2,1)S(1)}, u32[]{:S(2)}, u32[]{:S(2)}) collective-permute-start(bf16[8,72,768]{2,1,0:T(8,128)(2,1)S(1)} %bitcast.110), channel_id=1, source_target_pairs={{0,8},{4,12},{8,0},{12,4},{16,24},{20,28},{24,16},{28,20},{1,9},{5... | collective-permute-start | bytes 2654216 | tf_op jit(solution)/shard_map/ppermute | solution.py:28
  178.1 21.9 %collective-permute-start.17 = (bf16[4,72,768]{2,1,0:T(8,128)(2,1)S(1)}, bf16[4,72,768]{2,1,0:T(8,128)(2,1)S(1)}, u32[]{:S(2)}, u32[]{:S(2)}) collective-permute-start(bf16[4,72,768]{2,1,0:T(8,128)(2,1)S(1)} %get-tuple-element.285), channel_id=1, source_target_pairs={{0,16},{4,20},{8,24},{12,28},{16,0},{20,4},{24,8},{28,12},{1,17},{... | collective-permute-start | bytes 1327112 | tf_op jit(solution)/shard_map/ppermute | solution.py:28
  236.6 23.6 %collective-permute-start.24 = (bf16[1024,768]{1,0:T(8,128)(2,1)S(1)}, bf16[1024,768]{1,0:T(8,128)(2,1)S(1)}, u32[]{:S(2)}, u32[]{:S(2)}) collective-permute-start(bf16[1024,768]{1,0:T(8,128)(2,1)S(1)} %get-tuple-element.328), channel_id=1, source_target_pairs={{0,1},{1,0},{2,3},{3,2},{4,5},{5,4},{6,7},{7,6},{8,9},{9,8},{10,11... | collective-permute-start | bytes 4718600 | tf_op jit(solution)/shard_map/ppermute | solution.py:28
  236.8 22.0 %collective-permute-start.28 = (bf16[8,48,384]{2,1,0:T(8,128)(2,1)S(1)}, bf16[8,48,384]{2,1,0:T(8,128)(2,1)S(1)}, u32[]{:S(2)}, u32[]{:S(2)}) collective-permute-start(bf16[8,48,384]{2,1,0:T(8,128)(2,1)S(1)} %bitcast.115), channel_id=1, source_target_pairs={{0,2},{1,3},{2,0},{3,1},{4,6},{5,7},{6,4},{7,5},{8,10},{9,11},{10,... | collective-permute-start | bytes 884744 | tf_op jit(solution)/shard_map/ppermute | solution.py:28
  239.5 19.3 %collective-permute-start.29 = (bf16[8,48,384]{2,1,0:T(8,128)(2,1)S(1)}, bf16[8,48,384]{2,1,0:T(8,128)(2,1)S(1)}, u32[]{:S(2)}, u32[]{:S(2)}) collective-permute-start(bf16[8,48,384]{2,1,0:T(8,128)(2,1)S(1)} %bitcast.114), channel_id=1, source_target_pairs={{0,4},{4,0},{8,12},{12,8},{16,20},{20,16},{24,28},{28,24},{1,5},{5... | collective-permute-start | bytes 884744 | tf_op jit(solution)/shard_map/ppermute | solution.py:28
  239.5 19.3 %collective-permute-start.30 = (bf16[8,48,384]{2,1,0:T(8,128)(2,1)S(1)}, bf16[8,48,384]{2,1,0:T(8,128)(2,1)S(1)}, u32[]{:S(2)}, u32[]{:S(2)}) collective-permute-start(bf16[8,48,384]{2,1,0:T(8,128)(2,1)S(1)} %bitcast.113), channel_id=1, source_target_pairs={{0,8},{4,12},{8,0},{12,4},{16,24},{20,28},{24,16},{28,20},{1,9},{5... | collective-permute-start | bytes 884744 | tf_op jit(solution)/shard_map/ppermute | solution.py:28
  262.2 19.3 %collective-permute-start.62 = (bf16[2,72,768]{2,1,0:T(8,128)(2,1)S(1)}, bf16[2,72,768]{2,1,0:T(8,128)(2,1)S(1)}, u32[]{:S(2)}, u32[]{:S(2)}) collective-permute-start(bf16[2,72,768]{2,1,0:T(8,128)(2,1)S(1)} %get-tuple-element.412.refs_2_), channel_id=1, source_target_pairs={{0,8},{4,12},{8,0},{12,4},{16,24},{20,28},{24,16},{28,20},{1,9},{5... | collective-permute-start | bytes 663560 | tf_op jit(solution)/shard_map/ppermute | solution.py:28
  282.2 31.6 %collective-permute-start.64 = (bf16[4,72,768]{2,1,0:T(8,128)(2,1)S(1)}, bf16[4,72,768]{2,1,0:T(8,128)(2,1)S(1)}, u32[]{:S(2)}, u32[]{:S(2)}) collective-permute-start(bf16[4,72,768]{2,1,0:T(8,128)(2,1)S(1)} %get-tuple-element.417.refs_0_), channel_id=1, source_target_pairs={{0,4},{4,0},{8,12},{12,8},{16,20},{20,16},{24,28},{28,24},{1,5},{5... | collective-permute-start | bytes 1327112 | tf_op jit(solution)/shard_map/ppermute | solution.py:28
  289.4 26.4 %collective-permute-start.65 = (bf16[4,72,768]{2,1,0:T(8,128)(2,1)S(1)}, bf16[4,72,768]{2,1,0:T(8,128)(2,1)S(1)}, u32[]{:S(2)}, u32[]{:S(2)}) collective-permute-start(bf16[4,72,768]{2,1,0:T(8,128)(2,1)S(1)} %get-tuple-element.418.refs_2_), channel_id=1, source_target_pairs={{0,2},{1,3},{2,0},{3,1},{4,6},{5,7},{6,4},{7,5},{8,10},{9,11},{10,... | collective-permute-start | bytes 1327112 | tf_op jit(solution)/shard_map/ppermute | solution.py:28
  293.0 24.2 %collective-permute-start.66 = (bf16[4,72,768]{2,1,0:T(8,128)(2,1)S(1)}, bf16[4,72,768]{2,1,0:T(8,128)(2,1)S(1)}, u32[]{:S(2)}, u32[]{:S(2)}) collective-permute-start(bf16[4,72,768]{2,1,0:T(8,128)(2,1)S(1)} %get-tuple-element.419.refs_4_), channel_id=1, source_target_pairs={{0,16},{4,20},{8,24},{12,28},{16,0},{20,4},{24,8},{28,12},{1,17},{... | collective-permute-start | bytes 1327112 | tf_op jit(solution)/shard_map/ppermute | solution.py:28
  318.0 55.3 %collective-permute-start.67 = (bf16[8,72,768]{2,1,0:T(8,128)(2,1)S(1)}, bf16[8,72,768]{2,1,0:T(8,128)(2,1)S(1)}, u32[]{:S(2)}, u32[]{:S(2)}) collective-permute-start(bf16[8,72,768]{2,1,0:T(8,128)(2,1)S(1)} %get-tuple-element.423.refs_0_), channel_id=1, source_target_pairs={{0,2},{1,3},{2,0},{3,1},{4,6},{5,7},{6,4},{7,5},{8,10},{9,11},{10,... | collective-permute-start | bytes 2654216 | tf_op jit(solution)/shard_map/ppermute | solution.py:28
  322.1 52.1 %collective-permute-start.68 = (bf16[8,72,768]{2,1,0:T(8,128)(2,1)S(1)}, bf16[8,72,768]{2,1,0:T(8,128)(2,1)S(1)}, u32[]{:S(2)}, u32[]{:S(2)}) collective-permute-start(bf16[8,72,768]{2,1,0:T(8,128)(2,1)S(1)} %get-tuple-element.424.refs_2_), channel_id=1, source_target_pairs={{0,4},{4,0},{8,12},{12,8},{16,20},{20,16},{24,28},{28,24},{1,5},{5... | collective-permute-start | bytes 2654216 | tf_op jit(solution)/shard_map/ppermute | solution.py:28
  322.9 52.4 %collective-permute-start.69 = (bf16[8,72,768]{2,1,0:T(8,128)(2,1)S(1)}, bf16[8,72,768]{2,1,0:T(8,128)(2,1)S(1)}, u32[]{:S(2)}, u32[]{:S(2)}) collective-permute-start(bf16[8,72,768]{2,1,0:T(8,128)(2,1)S(1)} %get-tuple-element.425.refs_4_), channel_id=1, source_target_pairs={{0,8},{4,12},{8,0},{12,4},{16,24},{20,28},{24,16},{28,20},{1,9},{5... | collective-permute-start | bytes 2654216 | tf_op jit(solution)/shard_map/ppermute | solution.py:28
  326.2 54.3 %collective-permute-start.5 = (bf16[512,768]{1,0:T(8,128)(2,1)S(1)}, bf16[512,768]{1,0:T(8,128)(2,1)S(1)}, u32[]{:S(2)}, u32[]{:S(2)}) collective-permute-start(bf16[512,768]{1,0:T(8,128)(2,1)S(1)} %dynamic-slice_bitcast_fusion), channel_id=1, source_target_pairs={{0,2},{1,3},{2,0},{3,1},{4,6},{5,7},{6,4},{7,5},{8,10},{9,11},{10,... | collective-permute-start | bytes 2359304 | tf_op jit(solution)/shard_map/ppermute | solution.py:28
  380.5 43.5 %collective-permute-start.70 = (bf16[1152,768]{1,0:T(8,128)(2,1)}, bf16[1152,768]{1,0:T(8,128)(2,1)S(1)}, u32[]{:S(2)}, u32[]{:S(2)}) collective-permute-start(bf16[1152,768]{1,0:T(8,128)(2,1)} %bitcast.51.refs_1_), channel_id=1, source_target_pairs={{0,1},{1,0},{2,3},{3,2},{4,5},{5,4},{6,7},{7,6},{8,9},{9,8},{10,11... | collective-permute-start | bytes 5308424 | tf_op jit(solution)/shard_map/ppermute | solution.py:28
  380.5 43.5 %collective-permute-start.71 = (bf16[1152,768]{1,0:T(8,128)(2,1)}, bf16[1152,768]{1,0:T(8,128)(2,1)}, u32[]{:S(2)}, u32[]{:S(2)}) collective-permute-start(bf16[1152,768]{1,0:T(8,128)(2,1)} %bitcast.52.refs_2_), channel_id=1, source_target_pairs={{0,1},{1,0},{2,3},{3,2},{4,5},{5,4},{6,7},{7,6},{8,9},{9,8},{10,11... | collective-permute-start | bytes 5308424 | tf_op jit(solution)/shard_map/ppermute | solution.py:28
  381.0 43.0 %collective-permute-start.72 = (bf16[1152,768]{1,0:T(8,128)(2,1)}, bf16[1152,768]{1,0:T(8,128)(2,1)}, u32[]{:S(2)}, u32[]{:S(2)}) collective-permute-start(bf16[1152,768]{1,0:T(8,128)(2,1)} %bitcast.53.refs_3_), channel_id=1, source_target_pairs={{0,1},{1,0},{2,3},{3,2},{4,5},{5,4},{6,7},{7,6},{8,9},{9,8},{10,11... | collective-permute-start | bytes 5308424 | tf_op jit(solution)/shard_map/ppermute | solution.py:28
  387.7 19.9 %collective-permute-start.31 = (bf16[512,768]{1,0:T(8,128)(2,1)}, bf16[512,768]{1,0:T(8,128)(2,1)}, u32[]{:S(2)}, u32[]{:S(2)}) collective-permute-start(bf16[512,768]{1,0:T(8,128)(2,1)} %fusion.4), channel_id=1, source_target_pairs={{0,2},{1,3},{2,0},{3,1},{4,6},{5,7},{6,4},{7,5},{8,10},{9,11},{10,... | collective-permute-start | bytes 2359304 | tf_op jit(solution)/shard_map/ppermute | solution.py:28
  (120 other events, 1037.1 us)
